TPU v7x, 256 devices: a whole 4x4x8 slice. The times are simulated.
256 devices in a mesh: blk: 4 (over z_hi, core), grp: 64 (over y, z_lo, x).
Axes of the slice: x: 4, y: 4, z: 8 (z_hi: 2, z_lo: 4; z = z_hi * 4 + z_lo), core: 2. Of those that a mesh axis runs over, the one named last changes fastest.
Arguments:
- design: float32 [8, 32768], P(None, ('blk', 'grp')), may hold values from -5 to 5
- lengthscales: float32 [8], replicated, may hold values from 0.55 to 0.85
- counts: int32 [32768], P(('blk', 'grp')), may hold values from 1 to 16
- noise_base: float32 [1], replicated, may hold values from 0.5 to 2
- targets: float32 [16, 32768], P(None, ('blk', 'grp')), may hold values from -6 to 6
Outputs:
- solution: float32 [16, 32768], P(None, ('blk', 'grp'))
- residual: float32 [16, 32768], P(None, ('blk', 'grp'))
- image: float32 [16, 32768], P(None, ('blk', 'grp'))
All inputs are finite; a program needn't handle non-finite values.
Results may differ from a plain program's by a relative error of at most 0.0003.
Values sent between devices are 32-bit elements; how exact they have to be, the bound alone decides.
A program may use at most 64 MiB of HBM per device.

v0:
```python
import math

import jax
import jax.numpy as jnp
from jax import lax
from jax.sharding import Mesh
from jax.sharding import PartitionSpec as P

GRP = ("grp_0", "grp_1", "grp_2")
BLK = ("blk_0", "blk_1")
BLK_GRP = ("blk_0", "blk_1", "grp_0", "grp_1", "grp_2")


ROOT_FIVE = 2.23606797749979


def sent_together(arrays, axis, dim, along):
    ends, at = ([], 0)
    for a in arrays[:-1]:
        at += a.shape[along]
        ends.append(at)
    both = jnp.concatenate(arrays, axis=along)
    return tuple(jnp.split(lax.all_gather(both, axis, axis=dim, tiled=True), ends, axis=along))


def one_axis_at_a_time(x, axes):
    for axis in axes:
        x = lax.psum(x, axis)
    return x


def kernel_terms(own_scaled, own_square, col_scaled, col_dirs, running):
    columns = col_scaled.shape[1]
    block_width = math.gcd(columns, 2048)
    block_count = columns // block_width

    def advance(block_index, partial_sum):
        offset = block_index * block_width
        chosen = lax.dynamic_slice_in_dim(col_scaled, offset, block_width, 1)
        chosen_dirs = lax.dynamic_slice_in_dim(col_dirs, offset, block_width, 1)
        chosen_square = jnp.sum(chosen * chosen, 0)
        inner_products = jnp.einsum(
            "dr,dc->rc", own_scaled, chosen, precision=lax.Precision.HIGHEST
        )
        dist_square = jnp.maximum(
            own_square[:, None] + chosen_square[None, :] - 2.0 * inner_products, 0.0
        )
        radius = jnp.sqrt(dist_square)
        kernel_tile = (1.0 + ROOT_FIVE * radius + 5.0 / 3.0 * dist_square) * jnp.exp(
            -ROOT_FIVE * radius
        )
        return partial_sum + jnp.einsum(
            "kc,rc->kr", chosen_dirs, kernel_tile, precision=lax.Precision.HIGHEST
        )

    return lax.fori_loop(0, block_count, advance, running)


def on_device(design, lengthscales, counts, noise_base, targets):
    scaled = design / lengthscales[:, None]
    own_square = jnp.sum(scaled * scaled, 0)
    noise_diag = noise_base[0] / counts.astype(jnp.float32)

    def operator_apply(direction):
        zero_start = jnp.zeros(direction.shape, jnp.float32)
        group_points, group_dirs = sent_together((scaled, direction), GRP, 1, 0)
        portions = sent_together((group_points, group_dirs), BLK, 1, 0)
        product_sum = kernel_terms(scaled, own_square, portions[0], portions[1], zero_start)
        return product_sum + noise_diag[None, :] * direction

    first = operator_apply(targets)
    local_gammas = jnp.sum(targets * targets, 1)
    local_deltas = jnp.sum(first * targets, 1)
    gammas, deltas = (
        one_axis_at_a_time(local_gammas, BLK_GRP),
        one_axis_at_a_time(local_deltas, BLK_GRP),
    )
    further = operator_apply(first)
    alphas = (gammas / deltas)[:, None]
    solution = alphas * targets
    residual = targets - alphas * first
    image = first - alphas * further
    return (solution, residual, image)


def solution(mesh):
    split = Mesh(mesh.devices.reshape(2, 2, 4, 4, 4), ("blk_0", "blk_1", "grp_0", "grp_1", "grp_2"))
    placed = (P(None, BLK_GRP), P(), P(BLK_GRP), P(), P(None, BLK_GRP))
    return jax.shard_map(
        on_device,
        mesh=split,
        in_specs=placed,
        out_specs=(P(None, BLK_GRP), P(None, BLK_GRP), P(None, BLK_GRP)),
        check_vma=False,
    )
```

profile of v0, /device:TPU:1, one launch (start us, length us, event | category | flops | bytes accessed | tf_op | source)
XLA Modules:
  0.0 652.3 jit_solution(3243775043664825612)
XLA Ops:
  8.7 175.0 %all_gather.12 = f32[24,8192]{1,0:T(8,128)} all-gather(f32[24,128]{1,0:T(8,128)S(1)} %pad_maximum_fusion.1), channel_id=1, replica_groups=mesh['blk_0'=2,'blk_1'=2,'grp_0'=4,'grp_1'=4,'grp_2'=4] {'grp_0','grp_1'..., dimensions={1}, use_global_device_ids=true | all-gather | bytes 798720 | tf_op jit(solution)/shard_map/all_gather | solution.py:23
  185.1 77.0 %all-gather.3.cloned.1.call-done = f32[24,32768]{1,0:T(8,128)} async-done(((f32[24,8192]{1,0:T(8,128)}), f32[24,32768]{1,0:T(8,128)}) %all-gather.3.cloned.1.call-update) | async-done | bytes 3145744 | tf_op jit(solution)/shard_map/all_gather | solution.py:23
  262.0 3.1 split.20
  266.4 65.4 %while.28 = (s32[]{:T(128)}, f32[16,128]{1,0:T(8,128)S(1)}, f32[16,32768]{1,0:T(8,128)}, f32[128]{0:T(128)S(1)}, f32[8,32768]{1,0:T(8,128)S(1)}, /*index=5*/f32[...) while((s32[]{:T(128)}, f32[16,128]{1,0:T(8,128)S(1)}, f32[16,32768]{1,0:T(8,128)}, ...), condition=%wide.region_9.0_spmd.clone, body=%wide.region_7.9_spmd.clone.sunk | while | flops 78153728 | bytes 2396841 | solution.py:56
  268.4 2.0 convolution_add_fusion.4
  276.6 2.0 convolution_add_fusion.4
  280.6 2.0 convolution_add_fusion.4
  284.7 2.0 convolution_add_fusion.4
  297.0 2.0 convolution_add_fusion.4
  301.1 2.0 convolution_add_fusion.4
  305.2 2.0 convolution_add_fusion.4
  313.3 2.0 convolution_add_fusion.4
  317.4 2.0 convolution_add_fusion.4
  321.5 2.0 convolution_add_fusion.4
  325.6 2.0 convolution_add_fusion.4
  331.9 169.1 %all_gather.14 = f32[24,8192]{1,0:T(8,128)} all-gather(f32[24,128]{1,0:T(8,128)S(1)} %pad_maximum_fusion), channel_id=1, replica_groups=mesh['blk_0'=2,'blk_1'=2,'grp_0'=4,'grp_1'=4,'grp_2'=4] {'grp_0','grp_1'..., dimensions={1}, use_global_device_ids=true | all-gather | bytes 798720 | tf_op jit(solution)/shard_map/all_gather | solution.py:23
  501.0 7.7 %all-reduce.4 = (f32[16]{0:T(128)S(1)}, f32[16]{0:T(128)S(1)}) all-reduce(f32[16]{0:T(128)S(1)} %get-tuple-element.266, f32[16]{0:T(128)S(1)} %get-tuple-element.265), channel_id=1, replica_groups=mesh['blk_0'=2,'blk_1'=2,'grp_0'=4,'grp_1'=4,'grp_2'=4] {'blk_0'}, use_global_device_ids=true, to_apply=%region_1.2 | all-reduce | flops 32 | bytes 256 | tf_op jit(solution)/shard_map/psum | solution.py:28
  508.7 30.9 %all-reduce.3 = (f32[16]{0:T(128)S(1)}, f32[16]{0:T(128)S(1)}) all-reduce(f32[16]{0:T(128)S(1)} %get-tuple-element.299, f32[16]{0:T(128)S(1)} %get-tuple-element.300), channel_id=1, replica_groups=mesh['blk_0'=2,'blk_1'=2,'grp_0'=4,'grp_1'=4,'grp_2'=4] {'blk_1'}, use_global_device_ids=true, to_apply=%region_2.3 | all-reduce | flops 32 | bytes 256 | tf_op jit(solution)/shard_map/psum | solution.py:28
  539.7 6.8 %all-reduce.2 = (f32[16]{0:T(128)S(1)}, f32[16]{0:T(128)S(1)}) all-reduce(f32[16]{0:T(128)S(1)} %get-tuple-element.297, f32[16]{0:T(128)S(1)} %get-tuple-element.298), channel_id=1, replica_groups=mesh['blk_0'=2,'blk_1'=2,'grp_0'=4,'grp_1'=4,'grp_2'=4] {'grp_0'}, use_global_device_ids=true, to_apply=%region_3.0 | all-reduce | flops 32 | bytes 256 | tf_op jit(solution)/shard_map/psum | solution.py:28
  546.4 9.7 %all-reduce.1 = (f32[16]{0:T(128)S(1)}, f32[16]{0:T(128)S(1)}) all-reduce(f32[16]{0:T(128)S(1)} %get-tuple-element.295, f32[16]{0:T(128)S(1)} %get-tuple-element.296), channel_id=1, replica_groups=mesh['blk_0'=2,'blk_1'=2,'grp_0'=4,'grp_1'=4,'grp_2'=4] {'grp_1'}, use_global_device_ids=true, to_apply=%region_4.0 | all-reduce | flops 32 | bytes 256 | tf_op jit(solution)/shard_map/psum | solution.py:28
  556.1 6.8 %all-reduce = (f32[16]{0:T(128)S(1)}, f32[16]{0:T(128)S(1)}) all-reduce(f32[16]{0:T(128)S(1)} %get-tuple-element.293, f32[16]{0:T(128)S(1)} %get-tuple-element.294), channel_id=1, replica_groups=mesh['blk_0'=2,'blk_1'=2,'grp_0'=4,'grp_1'=4,'grp_2'=4] {'grp_2'}, use_global_device_ids=true, to_apply=%region_5.0 | all-reduce | flops 32 | bytes 256 | tf_op jit(solution)/shard_map/psum | solution.py:28
  562.9 12.2 %all-gather.5.cloned.1.call-done = f32[24,32768]{1,0:T(8,128)} async-done(((f32[24,8192]{1,0:T(8,128)}), f32[24,32768]{1,0:T(8,128)}) %all-gather.5.cloned.1.call-update) | async-done | bytes 3145744 | tf_op jit(solution)/shard_map/all_gather | solution.py:23
  575.1 3.1 split.22
  579.4 65.4 %while.29 = (s32[]{:T(128)}, f32[16,128]{1,0:T(8,128)S(1)}, f32[16,32768]{1,0:T(8,128)}, f32[128]{0:T(128)S(1)}, f32[8,32768]{1,0:T(8,128)S(1)}, /*index=5*/f32[...) while((s32[]{:T(128)}, f32[16,128]{1,0:T(8,128)S(1)}, f32[16,32768]{1,0:T(8,128)}, ...), condition=%wide.region_18.0_spmd.clone, body=%wide.region_16.0_spmd.clone.sunk | while | flops 78153728 | bytes 2396841 | solution.py:56
  (104 shorter events, 112.5 us)
Async XLA Ops:
  7.2 254.9 %all-gather.3.cloned.1.call-start = ((), (), s32[]{:S(2)}) async-start(), calls=%async_computation | async-start | bytes 3932160 | tf_op jit(solution)/shard_map/all_gather | solution.py:23
  183.7 391.4 %all-gather.5.cloned.1.call-start = ((), (), s32[]{:S(2)}) async-start(), calls=%async_computation.1 | async-start | bytes 3932160 | tf_op jit(solution)/shard_map/all_gather | solution.py:23
  265.1 1.2 slice-start.1
  266.4 65.4 %copy-start = (f32[16,128]{1,0:T(8,128)S(1)}, f32[16,128]{1,0:T(8,128)}, u32[]{:S(2)}) copy-start(f32[16,128]{1,0:T(8,128)} %param.13) | copy-start | bytes 24580
  578.2 1.2 slice-start
Sparse Core Ops, SparseCore 0:
  183.8 78.1 all-gather.2
  501.1 73.9 all-gather.4
where the time goes:
time: 655 us; the launch traced here: 652 us
  blocking collectives  406 us (62%)
  matrix products  128 us (20%)
  waiting for transfers between devices  89.2 us (14%)
  between operations  14.7 us (2%)
  local copies, waits for them, and re-layouts  8.64 us (1%)
    all_gather x2, blocking collectives, sent_together(): lax.all_gather(both, axis, axis=dim, tiled=True)  344 us
    all_gather x2, waiting for transfers between devices, sent_together(): lax.all_gather(both, axis, axis=dim, tiled=True)  89.2 us
    dot_general x32, matrix products, advance(): jnp.einsum('kc,rc->kr', chosen_dirs, kernel_tile, precision=lax.Precision...  64.9 us
    dot_general x32, matrix products, advance(): jnp.einsum('dr,dc->rc', own_scaled, chosen, precision=lax.Precision.HIGHEST)  63.5 us
    psum x5, blocking collectives, one_axis_at_a_time(): x = lax.psum(x, axis)  61.9 us
  transfers between devices with their start and end apart: 2, of which 2 were waited for; matrix products, arithmetic and copies ran while one was open for 0% of the time, Pallas kernels for 0%

commit v1 on v0

v1 whole, which is shorter than its diff:
```python
import functools

import jax
import jax.numpy as jnp
from jax import lax
from jax.experimental import pallas as pl
from jax.experimental.pallas import tpu as pltpu
from jax.sharding import PartitionSpec as P

MESH = pl.DeviceIdType.MESH
F32, BF16 = jnp.float32, jnp.bfloat16

NRHS = 16
CH = 128
SCALE = 2.23606797749979 * 1.4426950408889634
QUAD = 0.6931471805599453**2 / 3.0
LIN = 0.6931471805599453 / QUAD
ONE = 1.0 / QUAD
TINY = 1e-30

COLS = ((0, 0), (0, 2), (2, 0), (2, 2), (0, 1), (1, 0), (1, 1), (1, 3), (1, 2), (2, 1), (0, 3), (3, 0), (3, 3), (3, 1), (3, 2), (2, 3))
ROWS = ((0, 0), (0, 1), (4, 0), (4, 1), (1, 0), (7, 1), (2, 0), (6, 1), (3, 0), (5, 1))
NC, NR = len(COLS), len(ROWS)
HALF = 10
TILE = 256


def hops(offset, sizes):
    return sum(min(d, s - d) for d, s in zip(offset, sizes))


COL_ORDER = sorted(range(1, NC), key=lambda s: -hops(COLS[s], (4, 4)))
ROW_ORDER = sorted(range(1, NR), key=lambda s: -hops(ROWS[s], (8, 1)))


def three_parts(x):
    h = x.astype(BF16).astype(F32)
    m = (x - h).astype(BF16).astype(F32)
    return h, m, (x - h - m).astype(BF16).astype(F32)


def features(points, own):
    h, m, l = three_parts(points)
    qh, qm, ql = three_parts(jnp.sum(points * points, 0, keepdims=True))
    row = lax.broadcasted_iota(jnp.int32, points.shape, 0)
    first = 0 if own else 3
    q = jnp.where(row == first, qh, jnp.where(row == first + 1, qm, jnp.where(row == first + 2, ql, jnp.where(row < 6, 1.0, 0.0))))
    zero = jnp.zeros_like(points)
    if own:
        return jnp.concatenate([h, h, m, h, l, m, q, zero], 0)
    h, m, l = -2.0 * h, -2.0 * m, -2.0 * l
    return jnp.concatenate([h, m, h, l, h, m, q, zero], 0)


def kernel_values(d):
    d = jnp.maximum(d, TINY)
    u = d * lax.rsqrt(d)
    return (d + u * LIN + ONE) * jnp.exp2(-u)


def dot(a, b, ca, cb):
    return lax.dot_general(a, b, (((ca,), (cb,)), ((), ())), preferred_element_type=F32)


def folded(y):
    return y[:NRHS] + y[NRHS:]


def split32(v):
    h = v.astype(BF16)
    return jnp.concatenate([h, (v - h.astype(F32)).astype(BF16)], 0)


def cg_kernel(
    design_ref, scales_ref, counts_ref, noise_ref, targets_ref,
    sol_ref, res_ref, img_ref,
    pc, pr, vc2, vr2, txr, txc, rxr, rxc, tot, rtot,
    fa, fb, vc, vr, khi, klo, ycol, y1,
    lsem, pcs, pcr, prs, prr, vcs, vcr, vrs, vrr, txrs, rxrs, txcs, rxcs, tots, totr,
):
    blk, grp = lax.axis_index("blk"), lax.axis_index("grp")
    z, core = (blk // 2) * 4 + (grp // 4) % 4, blk % 2
    y, x = grp // 16, grp % 4

    def col_peer(slot, sign):
        dx, dy = COLS[slot]
        px, py = (x + (sign * dx) % 4) % 4, (y + (sign * dy) % 4) % 4
        return (blk, py * 16 + (z % 4) * 4 + px)

    def row_at(dz, dc):
        pz, pcore = (z + dz % 8) % 8, (core + dc) % 2
        return ((pz // 4) * 2 + pcore, y * 16 + (pz % 4) * 4 + x)

    def row_peer(slot, sign):
        dz, dc = ROWS[slot]
        return row_at(sign * dz, dc)

    others = [(dz, dc) for dz in range(8) for dc in range(2) if (dz, dc) != (0, 0)]

    local = [
        pltpu.make_async_copy(design_ref, pc.at[0, 0:8], lsem.at[0]),
        pltpu.make_async_copy(targets_ref, pc.at[0, 8:24], lsem.at[1]),
        pltpu.make_async_copy(design_ref, pr.at[0, 0:8], lsem.at[2]),
        pltpu.make_async_copy(targets_ref, pr.at[0, 8:24], lsem.at[3]),
    ]
    for c in local:
        c.start()

    barrier = pltpu.get_barrier_semaphore()
    for dz, dc in others:
        pl.semaphore_signal(barrier, inc=1, device_id=row_at(dz, dc), device_id_type=MESH)
    for slot in range(1, NC):
        pl.semaphore_signal(barrier, inc=1, device_id=col_peer(slot, 1), device_id_type=MESH)
    for c in local:
        c.wait()
    pl.semaphore_wait(barrier, len(others) + NC - 1)

    def remote(src, dst, ssem, rsem, peer):
        return pltpu.make_async_remote_copy(src_ref=src, dst_ref=dst, send_sem=ssem, recv_sem=rsem, device_id=peer, device_id_type=MESH)

    gather = [remote(pc.at[0], pc.at[s], pcs.at[s], pcr.at[s], col_peer(s, -1)) for s in COL_ORDER]
    gather += [remote(pc.at[0], pr.at[s], prs.at[s], prr.at[s], row_peer(s, -1)) for s in ROW_ORDER]
    for c in gather:
        c.start()

    lane8 = lax.broadcasted_iota(jnp.int32, (8, CH), 0)
    scales = jnp.zeros((8, CH), F32)
    for d in range(8):
        scales = jnp.where(lane8 == d, scales_ref[d], scales)
    noise = noise_ref[0] / counts_ref[...].astype(F32)

    for c in gather:
        c.wait()

    for s in range(NC):
        at = slice(s * CH, (s + 1) * CH)
        fb[:, at] = features(pc[s, 0:8] / scales * SCALE, False).astype(BF16)
        vc[:, at] = split32(pc[s, 8:24])
    for s in range(NR):
        at = slice(s * CH, (s + 1) * CH)
        fa[at, :] = features(pr[s, 0:8] / scales * SCALE, True).T.astype(BF16)
        vr[:, at] = split32(pr[s, 8:24])

    def tile(r, c, first_pass):
        rows, cols = slice(r, r + TILE), slice(c, c + TILE)
        if not first_pass:
            return khi[rows, cols], klo[rows, cols]
        k = kernel_values(dot(fa[rows, :], fb[:, cols], 1, 0))
        hi = k.astype(BF16)
        lo = (k - hi.astype(F32)).astype(BF16)
        khi[rows, cols] = hi
        klo[rows, cols] = lo
        return hi, lo

    def apply(first_pass, p):
        ycol[...] = jnp.zeros_like(ycol)
        sends = []
        for r0 in (2, 0, 8, 6, 4):
            half = r0 < 4
            r = r0 * CH
            rows = slice(r, r + TILE)
            yrow = jnp.zeros((NRHS, TILE), F32)
            for c in range(0, (HALF if half else NC) * CH, TILE):
                cols = slice(c, c + TILE)
                hi, lo = tile(r, c, first_pass)
                yrow += folded(dot(vc[:, cols], hi, 1, 1)) + dot(vc[0:NRHS, cols], lo, 1, 1)
                if not half or c >= 4 * CH:
                    ycol[:, cols] += folded(dot(vr[:, rows], hi, 1, 0)) + dot(vr[0:NRHS, rows], lo, 1, 0)
            for s in (r0, r0 + 1):
                txr[p, s] = yrow[:, (s - r0) * CH : (s - r0 + 1) * CH]
                if s:
                    c = remote(txr.at[p, s], rxr.at[p, s], txrs.at[p, s], rxrs.at[p, s], row_peer(s, 1))
                    c.start()
                    sends.append(c)
        for s in COL_ORDER:
            txc[p, s] = ycol[:, s * CH : (s + 1) * CH]
            c = remote(txc.at[p, s], rxc.at[p, s], txcs.at[p, s], rxcs.at[p, s], col_peer(s, 1))
            c.start()
            sends.append(c)
        total = txr[p, 0] + ycol[:, 0:CH]
        for c in sends:
            c.wait()
        for s in range(1, NR):
            total += rxr[p, s]
        for s in range(1, NC):
            total += rxc[p, s]
        return total * QUAD

    own = pc[0, 8:24]
    first = apply(True, 0) + noise * own

    lane = lax.broadcasted_iota(jnp.int32, (NRHS, CH), 1)
    sub = lax.broadcasted_iota(jnp.int32, (NRHS, CH), 0)
    gamma = jnp.sum(own * own, 1, keepdims=True)
    delta = jnp.sum(first * own, 1, keepdims=True)
    marked = jnp.where(lane == sub, gamma, 0.0) + jnp.where(lane == sub + NRHS, delta, 0.0)
    stats = jnp.sum(marked, 0, keepdims=True)

    y1[...] = first
    vc2[0, 0:16] = first
    vc2[0, 16:24] = jnp.broadcast_to(stats, (8, CH))
    vr2[0] = first
    gather = [remote(vc2.at[0], vc2.at[s], vcs.at[s], vcr.at[s], col_peer(s, -1)) for s in COL_ORDER]
    gather += [remote(vr2.at[0], vr2.at[s], vrs.at[s], vrr.at[s], row_peer(s, -1)) for s in ROW_ORDER]
    for c in gather:
        c.start()
    for c in gather:
        c.wait()

    group_stats = vc2[0, 16:24]
    for s in range(1, NC):
        group_stats += vc2[s, 16:24]
    tot[...] = group_stats
    exchange = [remote(tot, rtot.at[i], tots.at[i], totr.at[i], row_at(dz, dc)) for i, (dz, dc) in enumerate(others)]
    for c in exchange:
        c.start()

    for s in range(NC):
        vc[:, s * CH : (s + 1) * CH] = split32(vc2[s, 0:16])
    for s in range(NR):
        vr[:, s * CH : (s + 1) * CH] = split32(vr2[s])
    further = apply(False, 1) + noise * y1[...]

    for c in exchange:
        c.wait()
    for i in range(len(others)):
        group_stats += rtot[i]
    spread = jnp.broadcast_to(group_stats[0:1], (NRHS, CH))
    gammas = jnp.sum(jnp.where(lane == sub, spread, 0.0), 1, keepdims=True)
    deltas = jnp.sum(jnp.where(lane == sub + NRHS, spread, 0.0), 1, keepdims=True)
    alphas = gammas / deltas
    first = y1[...]
    sol_ref[...] = alphas * own
    res_ref[...] = own - alphas * first
    img_ref[...] = first - alphas * further


def on_device(design, lengthscales, counts, noise_base, targets):
    out = jax.ShapeDtypeStruct((NRHS, CH), F32)
    vmem, smem, anywhere = (pl.BlockSpec(memory_space=m) for m in (pltpu.VMEM, pltpu.SMEM, pl.ANY))
    dma = pltpu.SemaphoreType.DMA
    return pl.pallas_call(
        cg_kernel,
        out_shape=(out, out, out),
        in_specs=[anywhere, smem, vmem, smem, anywhere],
        out_specs=(vmem, vmem, vmem),
        scratch_shapes=[
            pltpu.VMEM((NC, 24, CH), F32),
            pltpu.VMEM((NR, 24, CH), F32),
            pltpu.VMEM((NC, 24, CH), F32),
            pltpu.VMEM((NR, NRHS, CH), F32),
            pltpu.VMEM((2, NR, NRHS, CH), F32),
            pltpu.VMEM((2, NC, NRHS, CH), F32),
            pltpu.VMEM((2, NR, NRHS, CH), F32),
            pltpu.VMEM((2, NC, NRHS, CH), F32),
            pltpu.VMEM((8, CH), F32),
            pltpu.VMEM((15, 8, CH), F32),
            pltpu.VMEM((NR * CH, 64), BF16),
            pltpu.VMEM((64, NC * CH), BF16),
            pltpu.VMEM((2 * NRHS, NC * CH), BF16),
            pltpu.VMEM((2 * NRHS, NR * CH), BF16),
            pltpu.VMEM((NR * CH, NC * CH), BF16),
            pltpu.VMEM((NR * CH, NC * CH), BF16),
            pltpu.VMEM((NRHS, NC * CH), F32),
            pltpu.VMEM((NRHS, CH), F32),
            dma((4,)),
            dma((NC,)), dma((NC,)), dma((NR,)), dma((NR,)),
            dma((NC,)), dma((NC,)), dma((NR,)), dma((NR,)),
            dma((2, NR)), dma((2, NR)), dma((2, NC)), dma((2, NC)),
            dma((15,)), dma((15,)),
        ],
        compiler_params=pltpu.CompilerParams(collective_id=0, has_side_effects=True, vmem_limit_bytes=48 << 20),
    )(design, lengthscales, counts.reshape(1, CH), noise_base, targets)


def solution(mesh):
    both = ("blk", "grp")
    placed = (P(None, both), P(), P(both), P(), P(None, both))
    out = P(None, both)
    return jax.shard_map(on_device, mesh=mesh, in_specs=placed, out_specs=(out, out, out), check_vma=False)
```

time: 655 us -> 53.7 us (0.08)
  blocking collectives: 406 us -> 0 us
  matrix products: 128 us -> 0 us
  waiting for transfers between devices: 89.2 us -> 0 us
  Pallas kernels: 0 us -> 48.3 us
  between operations: 14.7 us -> 1.31 us
    all_gather x2 -> x0, blocking collectives: 344 us -> none  [sent_together(): lax.all_gather(both, axis, axis=dim, tiled=True)]
    dot_general x64 -> x0, matrix products: 128 us -> none  [the longest x32 64.9 us: advance(): jnp.einsum('kc,rc->kr', chosen_dirs, kernel_tile, precision=lax.Precision...]
    all_gather x2 -> x0, waiting for transfers between devices: 89.2 us -> none  [sent_together(): lax.all_gather(both, axis, axis=dim, tiled=True)]
    psum x5 -> x0, blocking collectives: 61.9 us -> none  [one_axis_at_a_time(): x = lax.psum(x, axis)]
    pallas_call x0 -> x1, Pallas kernels: none -> 48.3 us  [on_device(): pl.pallas_call(cg_kernel, out_shape=(out, out, out), in_specs=[anywhere,...]
    split x6 -> x0, local copies, waits for them, and re-layouts: 8.64 us -> none  [sent_together(): jnp.split(lax.all_gather(both, axis, axis=dim, tiled=True), ends, axis=al...]
  transfers between devices with their start and end apart: 2 -> 0, of which waited for: 2 -> 0; matrix products, arithmetic and copies ran while one was open for 0% -> 0% of each run, Pallas kernels for 0% -> 0%
where the time goes in v1:
time: 53.7 us; the launch traced here: 53.5 us
  Pallas kernels  48.3 us (90%)
  local copies, waits for them, and re-layouts  3.84 us (7%)
  between operations  1.31 us (2%)
    pallas_call x1, Pallas kernels, on_device(): pl.pallas_call(cg_kernel, out_shape=(out, out, out), in_specs=[anywhere,...  48.3 us
    unnamed x11, local copies, waits for them, and re-layouts  3.84 us

profile of v1, /device:TPU:1, one launch (start us, length us, event | category | flops | bytes accessed | tf_op | source)
XLA Modules:
  0.0 53.5 jit_solution(6316458501750819711)
XLA Ops:
  1.3 0.0 copy-start.2
  1.3 0.0 copy-start.3
  1.3 0.6 %copy-done.2 = f32[8]{0:T(128)S(1)} copy-done((f32[8]{0:T(128)S(1)}, f32[8]{0:T(128)}, u32[]{:S(2)}) %copy-start.2) | copy-done | bytes 56
  1.9 0.0 copy-done.3
  1.9 0.0 copy-start
  2.0 0.7 %copy-done = f32[16,128]{1,0:T(8,128)S(1)} copy-done((f32[16,128]{1,0:T(8,128)S(1)}, f32[16,128]{1,0:T(8,128)}, u32[]{:S(2)}) %copy-start) | copy-done | bytes 8216
  2.6 0.0 copy-start.1
  2.6 0.7 %copy-done.1 = f32[8,128]{1,0:T(8,128)S(1)} copy-done((f32[8,128]{1,0:T(8,128)S(1)}, f32[8,128]{1,0:T(8,128)}, u32[]{:S(2)}) %copy-start.1) | copy-done | bytes 4120
  3.3 48.3 %shard_map.76 = (f32[16,128]{1,0:T(8,128)S(1)}, f32[16,128]{1,0:T(8,128)S(1)}, f32[16,128]{1,0:T(8,128)S(1)}) custom-call(f32[8,128]{1,0:T(8,128)S(1)} %copy-done.1, f32[8]{0:T(128)S(1)} %copy-done.2, s32[1,128]{1,0:T(1,128)S(1)} %bitcast.1, f32[1]{0:T(128)S(6)} %copy.11.noise_ref, f32[16,128]{1,0:T(8,128)S(1)} %copy-done), custom_call_target="tpu_custom_call" | custom-call | tf_op jit(solution)/shard_map/pallas_call | solution.py:242
  51.7 0.6 %copy.12 = f32[16,128]{1,0:T(8,128)} copy(f32[16,128]{1,0:T(8,128)S(1)} %get-tuple-element.6) | data formatting | bytes 16384
  52.3 0.6 %copy.13 = f32[16,128]{1,0:T(8,128)} copy(f32[16,128]{1,0:T(8,128)S(1)} %get-tuple-element.7) | data formatting | bytes 16384
  52.9 0.6 %copy.14 = f32[16,128]{1,0:T(8,128)} copy(f32[16,128]{1,0:T(8,128)S(1)} %get-tuple-element.8) | data formatting | bytes 16384
Async XLA Ops:
  1.3 0.7 %copy-start.2 = (f32[8]{0:T(128)S(1)}, f32[8]{0:T(128)}, u32[]{:S(2)}) copy-start(f32[8]{0:T(128)} %scales_ref.1) | copy-start | bytes 100
  1.3 0.7 %copy-start.3 = (s32[128]{0:T(128)S(1)}, s32[128]{0:T(128)}, u32[]{:S(2)}) copy-start(s32[128]{0:T(128)} %param.7) | copy-start | bytes 1540
  1.9 0.7 %copy-start = (f32[16,128]{1,0:T(8,128)S(1)}, f32[16,128]{1,0:T(8,128)}, u32[]{:S(2)}) copy-start(f32[16,128]{1,0:T(8,128)} %targets_ref.1) | copy-start | bytes 24580
  2.6 0.7 %copy-start.1 = (f32[8,128]{1,0:T(8,128)S(1)}, f32[8,128]{1,0:T(8,128)}, u32[]{:S(2)}) copy-start(f32[8,128]{1,0:T(8,128)} %design_ref.1) | copy-start | bytes 12292

commit v2 on v0

v2 whole, which is shorter than its diff:
```python
import functools

import jax
import jax.numpy as jnp
from jax import lax
from jax.experimental import pallas as pl
from jax.experimental.pallas import tpu as pltpu
from jax.sharding import PartitionSpec as P

MESH = pl.DeviceIdType.MESH
F32, BF16 = jnp.float32, jnp.bfloat16

NRHS = 16
CH = 128
SCALE = 2.23606797749979 * 1.4426950408889634
QUAD = 0.6931471805599453**2 / 3.0
LIN = 0.6931471805599453 / QUAD
ONE = 1.0 / QUAD
TINY = 1e-30

COLS = ((2, 2), (2, 0), (1, 2), (2, 1), (1, 1), (1, 3), (0, 0), (0, 2), (0, 1), (1, 0), (0, 3), (3, 0), (3, 3), (3, 1), (3, 2), (2, 3))
ROWS = ((0, 0), (0, 1), (4, 0), (4, 1), (1, 0), (7, 1), (2, 0), (6, 1), (3, 0), (5, 1))
NC, NR = len(COLS), len(ROWS)
OWN = COLS.index((0, 0))
TILE = 2 * CH
SUB = 64
HALF = (0, 1, 2, 3, 4)
ONE_WAY = (0, 3)
ROW_PEERS = tuple(sorted(((dz, dc) for dz in range(8) for dc in range(2) if dz or dc), key=lambda o: -min(o[0], 8 - o[0])))


def hops(offset, sizes):
    return sum(min(d, s - d) for d, s in zip(offset, sizes))


COL_ORDER = sorted((s for s in range(NC) if s != OWN), key=lambda s: -hops(COLS[s], (4, 4)))
ROW_ORDER = sorted(range(1, NR), key=lambda s: -hops(ROWS[s], (8, 1)))


def three_parts(x):
    h = x.astype(BF16).astype(F32)
    m = (x - h).astype(BF16).astype(F32)
    return h, m, (x - h - m).astype(BF16).astype(F32)


def features(points, own):
    h, m, l = three_parts(points)
    qh, qm, ql = three_parts(jnp.sum(points * points, 0, keepdims=True))
    row = lax.broadcasted_iota(jnp.int32, points.shape, 0)
    first = 0 if own else 3
    q = jnp.where(row == first, qh, jnp.where(row == first + 1, qm, jnp.where(row == first + 2, ql, jnp.where(row < 6, 1.0, 0.0))))
    zero = jnp.zeros_like(points)
    if own:
        return jnp.concatenate([h, h, m, h, l, m, q, zero], 0)
    h, m, l = -2.0 * h, -2.0 * m, -2.0 * l
    return jnp.concatenate([h, m, h, l, h, m, q, zero], 0)


def kernel_values(d):
    d = jnp.maximum(d, TINY)
    u = d * lax.rsqrt(d)
    return (d + u * LIN + ONE) * jnp.exp2(-u)


def dot(a, b, ca, cb):
    return lax.dot_general(a, b, (((ca,), (cb,)), ((), ())), preferred_element_type=F32)


def folded(y):
    return y[:NRHS] + y[NRHS:]


def split32(v):
    h = v.astype(BF16)
    return jnp.concatenate([h, (v - h.astype(F32)).astype(BF16)], 0)


def cg_kernel(
    design_ref, scales_ref, counts_ref, noise_ref, targets_ref,
    alpha_ref, first_ref, further_ref,
    scales_sm, noise_sm, counts_vm,
    dcol, drow, tcol, trow, fcol, frow, stats, tot, mine,
    txr, txc, rxr, rxc,
    fa, fb, vc, vr, khi, klo, yrow, ycol,
    lsem, ssem, dcr, drr, tcr, trr, fcr, frr, rxs, sts,
):
    blk, grp = lax.axis_index("blk"), lax.axis_index("grp")
    zh, core = lax.div(blk, 2), lax.rem(blk, 2)
    y, zl, x = lax.div(grp, 16), lax.rem(lax.div(grp, 4), 4), lax.rem(grp, 4)
    xs = [lax.rem(x + d, 4) for d in range(4)]
    ys = [lax.rem(y + d, 4) * 16 + zl * 4 for d in range(4)]
    zs = [lax.rem(zh * 4 + zl + d, 8) for d in range(8)]
    zblk = [lax.div(v, 4) * 2 for v in zs]
    zgrp = [lax.rem(v, 4) * 4 + y * 16 + x for v in zs]
    cores = [core, 1 - core]

    def col_at(dx, dy):
        return (blk, ys[dy % 4] + xs[dx % 4])

    def row_at(dz, dc):
        return (zblk[dz % 8] + cores[dc], zgrp[dz % 8])

    def col_peer(slot, sign):
        return col_at(sign * COLS[slot][0], sign * COLS[slot][1])

    def row_peer(slot, sign):
        return row_at(sign * ROWS[slot][0], ROWS[slot][1])

    barrier = pltpu.get_barrier_semaphore()
    for s in COL_ORDER:
        pl.semaphore_signal(barrier, inc=1, device_id=col_peer(s, 1), device_id_type=MESH)
    for o in ROW_PEERS:
        pl.semaphore_signal(barrier, inc=1, device_id=row_at(*o), device_id_type=MESH)

    local = [
        pltpu.make_async_copy(src, dst, lsem.at[i])
        for i, (src, dst) in enumerate((
            (scales_ref, scales_sm), (noise_ref, noise_sm), (counts_ref, counts_vm),
            (design_ref, dcol.at[OWN]), (design_ref, drow.at[0]), (targets_ref, tcol.at[OWN]), (targets_ref, trow.at[0]),
        ))
    ]
    for c in local:
        c.start()
    pl.semaphore_wait(barrier, len(COL_ORDER) + len(ROW_PEERS))

    def remote(src, dst, ssem_at, rsem, peer):
        return pltpu.make_async_remote_copy(
            src_ref=src, dst_ref=dst, send_sem=ssem.at[ssem_at], recv_sem=rsem, device_id=peer, device_id_type=MESH
        )

    def gather(src, col, col_sem, row, row_sem, at):
        order = [(hops(COLS[s], (4, 4)), 0, s) for s in COL_ORDER] + [(hops(ROWS[s], (8, 1)), 1, s) for s in ROW_ORDER]
        for _, is_row, s in sorted(order, key=lambda o: -o[0]):
            if is_row:
                remote(src, row.at[s], at + 1, row_sem.at[s // 2], row_peer(s, -1)).start()
            else:
                remote(src, col.at[s], at, col_sem.at[s // 2], col_peer(s, -1)).start()

    def pair_wait(buf, sem, pair, own):
        lo, hi = 2 * pair, 2 * pair + 2
        lo = lo + 1 if lo == own else lo
        remote(buf.at[lo:hi], buf.at[lo:hi], 0, sem.at[pair], col_peer(0, 1)).wait_recv()

    def sent(ref, at):
        remote(ref, ref, at, rxs.at[0, 0], col_peer(0, 1)).wait_send()

    gather(design_ref, dcol, dcr, drow, drr, 0)
    gather(targets_ref, tcol, tcr, trow, trr, 2)

    for c in local:
        c.wait()
    dim = lax.broadcasted_iota(jnp.int32, (8, CH), 0)
    scales = jnp.zeros((8, CH), F32)
    for d in range(8):
        scales = jnp.where(dim == d, scales_sm[d], scales)
    noise = noise_sm[0] / counts_vm[...].astype(F32)
    yrow[...] = jnp.zeros_like(yrow)
    ycol[...] = jnp.zeros_like(ycol)
    have = set()

    def need(key, wait, use):
        if key not in have:
            have.add(key)
            wait()
            use()

    def col_points(p):
        def use():
            for s in (2 * p, 2 * p + 1):
                fb[p, :, (s - 2 * p) * CH : (s - 2 * p + 1) * CH] = features(dcol[s] / scales * SCALE, False).astype(BF16)

        need(("dc", p), lambda: pair_wait(dcol, dcr, p, OWN), use)

    def row_points(r):
        def use():
            for s in (2 * r, 2 * r + 1):
                fa[r, (s - 2 * r) * CH : (s - 2 * r + 1) * CH, :] = features(drow[s] / scales * SCALE, True).T.astype(BF16)

        need(("dr", r), lambda: pair_wait(drow, drr, r, 0), use)

    def vectors(key, buf, sem, pair, own, out):
        def use():
            for s in (2 * pair, 2 * pair + 1):
                out[pair, :, (s - 2 * pair) * CH : (s - 2 * pair + 1) * CH] = split32(buf[s])

        need((key, pair), lambda: pair_wait(buf, sem, pair, own), use)

    def tile(r, p):
        for q in range(0, TILE, SUB):
            k = kernel_values(dot(fa[r, q : q + SUB, :], fb[p], 1, 0))
            hi = k.astype(BF16)
            khi[r, p, q : q + SUB, :] = hi
            klo[r, p, q : q + SUB, :] = (k - hi.astype(F32)).astype(BF16)

    def to_rows(r, p):
        yrow[r] += folded(dot(vc[p], khi[r, p], 1, 1)) + dot(vc[p, 0:NRHS], klo[r, p], 1, 1)

    def to_cols(r, p):
        if r > 1 or p not in ONE_WAY:
            ycol[p] += folded(dot(vr[r], khi[r, p], 1, 0)) + dot(vr[r, 0:NRHS], klo[r, p], 1, 0)

    def send_row(k, r):
        for s in (2 * r, 2 * r + 1):
            if s:
                txr[k, s - 1] = yrow[r, :, (s - 2 * r) * CH : (s - 2 * r + 1) * CH]
                remote(txr.at[k, s - 1], rxr.at[k, s - 1], 4 + 2 * k, rxs.at[k, 0], row_peer(s, 1)).start()

    def send_col(k, p):
        for s in (2 * p, 2 * p + 1):
            if s != OWN:
                i = s - (s > OWN)
                txc[k, i] = ycol[p, :, (s - 2 * p) * CH : (s - 2 * p + 1) * CH]
                remote(txc.at[k, i], rxc.at[k, i], 5 + 2 * k, rxs.at[k, 1], col_peer(s, 1)).start()

    def total(k):
        own = yrow[0, :, 0:CH] + ycol[OWN // 2, :, (OWN % 2) * CH : (OWN % 2 + 1) * CH]
        remote(rxr.at[k], rxr.at[k], 0, rxs.at[k, 0], col_peer(0, 1)).wait_recv()
        for i in range(NR - 1):
            own += rxr[k, i]
        remote(rxc.at[k], rxc.at[k], 0, rxs.at[k, 1], col_peer(0, 1)).wait_recv()
        for i in range(NC - 1):
            own += rxc[k, i]
        return own * QUAD

    jobs = [(0, p) for p in (4, 3, 2, 1, 0)] + [(1, p) for p in (0, 1, 2, 3, 4)] + [(4, p) for p in range(8)]
    col_last = (0, 7, 1, 6, 2, 5, 3, 4)
    jobs += [(r, p) for p in col_last for r in (3, 2)]
    lag = 3
    for i in range(len(jobs) + lag):
        if i < len(jobs):
            r, p = jobs[i]
            row_points(r)
            col_points(p)
            tile(r, p)
        if i >= lag:
            r, p = jobs[i - lag]
            vectors("tc", tcol, tcr, p, OWN, vc)
            vectors("tr", trow, trr, r, 0, vr)
            to_rows(r, p)
            to_cols(r, p)
            if i - lag == 4:
                send_row(0, 0)
            if i - lag == 9:
                send_row(0, 1)
            if i - lag == 17:
                send_row(0, 4)
            if i - lag >= 18 and r == 2:
                send_col(0, p)
    send_row(0, 3)
    send_row(0, 2)

    sent(dcol.at[0 : NC - 1], 0)
    sent(drow.at[0 : NR - 1], 1)
    sent(tcol.at[0 : NC - 1], 2)
    sent(trow.at[0 : NR - 1], 3)
    own = tcol[OWN]
    lane = lax.broadcasted_iota(jnp.int32, (NRHS, CH), 1)
    sub = lax.broadcasted_iota(jnp.int32, (NRHS, CH), 0)
    gamma = jnp.sum(own * own, 1, keepdims=True)
    first = total(0) + noise * own

    fcol[OWN] = first
    frow[0] = first
    gather(fcol.at[OWN], fcol, fcr, frow, frr, 8)

    delta = jnp.sum(first * own, 1, keepdims=True)
    marked = jnp.where(lane == sub, gamma, 0.0) + jnp.where(lane == sub + NRHS, delta, 0.0)
    mine[0] = jnp.sum(marked, 0, keepdims=True)
    for s in COL_ORDER:
        remote(mine.at[0], stats.at[s - (s > OWN)], 10, sts.at[0], col_peer(s, 1)).start()
    first_ref[...] = first
    yrow[...] = jnp.zeros_like(yrow)
    ycol[...] = jnp.zeros_like(ycol)

    def from_row(r):
        vectors("fr", frow, frr, r, 0, vr)
        for p in HALF if r < 2 else range(8):
            to_cols(r, p)

    def from_col(p):
        vectors("fc", fcol, fcr, p, OWN, vc)
        for r in range(5) if p in HALF else (2, 3, 4):
            to_rows(r, p)

    from_row(0)
    from_col(4)
    from_col(5)
    from_row(2)
    from_col(3)
    from_col(2)
    from_col(6)
    from_row(3)
    from_col(1)
    from_col(7)
    from_col(0)
    for r in (1, 4, 3, 2, 0):
        send_row(1, r)
    remote(stats, stats, 0, sts.at[0], col_peer(0, 1)).wait_recv()
    group = mine[0]
    for i in range(NC - 1):
        group += stats[i]
    mine[1] = group
    for i, o in enumerate(ROW_PEERS):
        remote(mine.at[1], tot.at[i], 11, sts.at[1], row_at(*o)).start()
    from_row(4)
    for p in (0, 7, 6, 3, 5):
        send_col(1, p)
    from_row(1)
    for p in (1, 2, 4):
        send_col(1, p)

    sent(txr.at[0], 4)
    sent(txc.at[0], 5)
    sent(fcol.at[0 : NC - 1], 8)
    sent(frow.at[0 : NR - 1], 9)
    sent(stats, 10)
    further_ref[...] = total(1) + noise * first_ref[...]
    remote(tot, tot, 0, sts.at[1], col_peer(0, 1)).wait_recv()
    for i in range(len(ROW_PEERS)):
        group += tot[i]
    spread = jnp.broadcast_to(group, (NRHS, CH))
    gammas = jnp.sum(jnp.where(lane == sub, spread, 0.0), 1, keepdims=True)
    deltas = jnp.sum(jnp.where(lane == sub + NRHS, spread, 0.0), 1, keepdims=True)
    alpha_ref[...] = jnp.broadcast_to(gammas / deltas, (NRHS, CH))
    sent(txr.at[1], 6)
    sent(txc.at[1], 7)
    sent(tot, 11)


def on_device(design, lengthscales, counts, noise_base, targets):
    out = jax.ShapeDtypeStruct((NRHS, CH), F32)
    vmem, hbm = (pl.BlockSpec(memory_space=m) for m in (pltpu.VMEM, pltpu.HBM))
    dma = pltpu.SemaphoreType.DMA

    def chunks(*shape):
        return pltpu.VMEM(shape + (CH,), F32)

    alphas, first, further = pl.pallas_call(
        cg_kernel,
        out_shape=(out, out, out),
        in_specs=[hbm] * 5,
        out_specs=(vmem, vmem, vmem),
        scratch_shapes=[
            pltpu.SMEM((8,), F32), pltpu.SMEM((1,), F32), pltpu.VMEM((1, CH), jnp.int32),
            chunks(NC, 8), chunks(NR, 8), chunks(NC, NRHS), chunks(NR, NRHS), chunks(NC, NRHS), chunks(NR, NRHS),
            chunks(NC - 1, 1), chunks(len(ROW_PEERS), 1), chunks(2, 1),
            chunks(2, NR - 1, NRHS), chunks(2, NC - 1, NRHS), chunks(2, NR - 1, NRHS), chunks(2, NC - 1, NRHS),
            pltpu.VMEM((NR // 2, TILE, 64), BF16), pltpu.VMEM((NC // 2, 64, TILE), BF16),
            pltpu.VMEM((NC // 2, 2 * NRHS, TILE), BF16), pltpu.VMEM((NR // 2, 2 * NRHS, TILE), BF16),
            pltpu.VMEM((NR // 2, NC // 2, TILE, TILE), BF16), pltpu.VMEM((NR // 2, NC // 2, TILE, TILE), BF16),
            pltpu.VMEM((NR // 2, NRHS, TILE), F32), pltpu.VMEM((NC // 2, NRHS, TILE), F32),
            dma((7,)), dma((12,)), dma((NC // 2,)), dma((NR // 2,)), dma((NC // 2,)), dma((NR // 2,)),
            dma((NC // 2,)), dma((NR // 2,)), dma((2, 2)), dma((2,)),
        ],
        compiler_params=pltpu.CompilerParams(collective_id=0, has_side_effects=True),
    )(design, lengthscales, counts.reshape(1, CH), noise_base, targets)
    return alphas * targets, targets - alphas * first, first - alphas * further


def solution(mesh):
    both = ("blk", "grp")
    placed = (P(None, both), P(), P(both), P(), P(None, both))
    out = P(None, both)
    return jax.shard_map(on_device, mesh=mesh, in_specs=placed, out_specs=(out, out, out), check_vma=False)
```

time: 655 us -> 48.4 us (0.07)
  blocking collectives: 406 us -> 0 us
  matrix products: 128 us -> 0 us
  waiting for transfers between devices: 89.2 us -> 0 us
  Pallas kernels: 0 us -> 45.6 us
  between operations: 14.7 us -> 1.3 us
  local copies, waits for them, and re-layouts: 8.64 us -> 0.01 us
    all_gather x2 -> x0, blocking collectives: 344 us -> none  [sent_together(): lax.all_gather(both, axis, axis=dim, tiled=True)]
    dot_general x64 -> x0, matrix products: 128 us -> none  [the longest x32 64.9 us: advance(): jnp.einsum('kc,rc->kr', chosen_dirs, kernel_tile, precision=lax.Precision...]
    all_gather x2 -> x0, waiting for transfers between devices: 89.2 us -> none  [sent_together(): lax.all_gather(both, axis, axis=dim, tiled=True)]
    psum x5 -> x0, blocking collectives: 61.9 us -> none  [one_axis_at_a_time(): x = lax.psum(x, axis)]
    pallas_call x0 -> x1, Pallas kernels: none -> 45.6 us  [on_device(): pl.pallas_call(cg_kernel, out_shape=(out, out, out), in_specs=[hbm] * 5,...]
    split x6 -> x0, local copies, waits for them, and re-layouts: 8.64 us -> none  [sent_together(): jnp.split(lax.all_gather(both, axis, axis=dim, tiled=True), ends, axis=al...]
  transfers between devices with their start and end apart: 2 -> 0, of which waited for: 2 -> 0; matrix products, arithmetic and copies ran while one was open for 0% -> 0% of each run, Pallas kernels for 0% -> 0%
where the time goes in v2:
time: 48.4 us; the launch traced here: 48.2 us
  Pallas kernels  45.6 us (94%)
  other arithmetic  1.34 us (3%)
  between operations  1.3 us (3%)
    pallas_call x1, Pallas kernels, on_device(): pl.pallas_call(cg_kernel, out_shape=(out, out, out), in_specs=[hbm] * 5,...  45.6 us
    sub x1, other arithmetic, on_device(): first - alphas * further  1.34 us

profile of v2, /device:TPU:1, one launch (start us, length us, event | category | flops | bytes accessed | tf_op | source)
XLA Modules:
  0.0 48.2 jit_solution(9617370842786129110)
XLA Ops:
  1.3 0.0 copy-start
  1.3 45.6 %shard_map.76 = (f32[16,128]{1,0:T(8,128)}, f32[16,128]{1,0:T(8,128)}, f32[16,128]{1,0:T(8,128)}) custom-call(f32[8,128]{1,0:T(8,128)} %design_ref.1, f32[8]{0:T(128)} %scales_ref.1, s32[1,128]{1,0:T(1,128)} %bitcast.1, f32[1]{0:T(128)S(6)} %copy.8.noise_ref, f32[16,128]{1,0:T(8,128)} %targets_ref.1), custom_call_target="tpu_custom_call" | custom-call | tf_op jit(solution)/shard_map/pallas_call | solution.py:338
  46.9 0.0 copy-done
  46.9 1.3 %multiply_subtract_fusion = (f32[16,128]{1,0:T(8,128)}, f32[16,128]{1,0:T(8,128)}, f32[16,128]{1,0:T(8,128)}) fusion(f32[16,128]{1,0:T(8,128)} %get-tuple-element.7, f32[16,128]{1,0:T(8,128)} %get-tuple-element.6, f32[16,128]{1,0:T(8,128)} %get-tuple-element.8, f32[16,128]{1,0:T(8,128)S(1)} %copy-done), kind=kLoop, calls=%fused_computation | loop fusion | flops 10240 | bytes 57344 | tf_op jit(solution)/shard_map/sub | solution.py:357
Async XLA Ops:
  1.3 45.6 %copy-start = (f32[16,128]{1,0:T(8,128)S(1)}, f32[16,128]{1,0:T(8,128)}, u32[]{:S(2)}) copy-start(f32[16,128]{1,0:T(8,128)} %targets_ref.1) | copy-start | bytes 24580

commit v3 on v2

--- a/solution.py
+++ b/solution.py
@@ -23,7 +23,13 @@
 NC, NR = len(COLS), len(ROWS)
 OWN = COLS.index((0, 0))
 TILE = 2 * CH
-SUB = 64
+LAG = 3
+JOBS = (
+    (0, 4), (0, 3), (0, 2), (2, 2), (2, 6), (3, 4), (3, 5), (3, 3), (3, 2), (3, 6),
+    (1, 0), (1, 1), (1, 2), (1, 3), (1, 4), (4, 0), (0, 0), (2, 0), (3, 0), (4, 7), (2, 7), (3, 7),
+    (4, 1), (0, 1), (2, 1), (3, 1), (4, 2), (4, 6), (4, 3), (4, 4), (4, 5), (2, 3), (2, 4), (2, 5),
+)
+STAGES = (((0, 2, 3), (4, 5, 3, 2, 6), 10), ((1, 4), (0, 1, 7), len(JOBS)))
 HALF = (0, 1, 2, 3, 4)
 ONE_WAY = (0, 3)
 ROW_PEERS = tuple(sorted(((dz, dc) for dz in range(8) for dc in range(2) if dz or dc), key=lambda o: -min(o[0], 8 - o[0])))
@@ -81,7 +87,7 @@
     scales_sm, noise_sm, counts_vm,
     dcol, drow, tcol, trow, fcol, frow, stats, tot, mine,
     txr, txc, rxr, rxc,
-    fa, fb, vc, vr, khi, klo, yrow, ycol,
+    fa, fb, vc, vr, ka, kb, la, lb, yrow, ycol,
     lsem, ssem, dcr, drr, tcr, trr, fcr, frr, rxs, sts,
 ):
     blk, grp = lax.axis_index("blk"), lax.axis_index("grp")
@@ -128,13 +134,14 @@
             src_ref=src, dst_ref=dst, send_sem=ssem.at[ssem_at], recv_sem=rsem, device_id=peer, device_id_type=MESH
         )
 
-    def gather(src, col, col_sem, row, row_sem, at):
+    def gather(*parts):
         order = [(hops(COLS[s], (4, 4)), 0, s) for s in COL_ORDER] + [(hops(ROWS[s], (8, 1)), 1, s) for s in ROW_ORDER]
-        for _, is_row, s in sorted(order, key=lambda o: -o[0]):
-            if is_row:
-                remote(src, row.at[s], at + 1, row_sem.at[s // 2], row_peer(s, -1)).start()
-            else:
-                remote(src, col.at[s], at, col_sem.at[s // 2], col_peer(s, -1)).start()
+        for _, is_row, s in sorted(order):
+            for src, col, col_sem, row, row_sem, at in parts:
+                if is_row:
+                    remote(src, row.at[s], at + 1, row_sem.at[s // 2], row_peer(s, -1)).start()
+                else:
+                    remote(src, col.at[s], at, col_sem.at[s // 2], col_peer(s, -1)).start()
 
     def pair_wait(buf, sem, pair, own):
         lo, hi = 2 * pair, 2 * pair + 2
@@ -144,8 +151,7 @@
     def sent(ref, at):
         remote(ref, ref, at, rxs.at[0, 0], col_peer(0, 1)).wait_send()
 
-    gather(design_ref, dcol, dcr, drow, drr, 0)
-    gather(targets_ref, tcol, tcr, trow, trr, 2)
+    gather((design_ref, dcol, dcr, drow, drr, 0), (targets_ref, tcol, tcr, trow, trr, 2))
 
     for c in local:
         c.wait()
@@ -156,48 +162,48 @@
     noise = noise_sm[0] / counts_vm[...].astype(F32)
     yrow[...] = jnp.zeros_like(yrow)
     ycol[...] = jnp.zeros_like(ycol)
-    have = set()
-
-    def need(key, wait, use):
-        if key not in have:
-            have.add(key)
-            wait()
-            use()
-
-    def col_points(p):
-        def use():
-            for s in (2 * p, 2 * p + 1):
-                fb[p, :, (s - 2 * p) * CH : (s - 2 * p + 1) * CH] = features(dcol[s] / scales * SCALE, False).astype(BF16)
-
-        need(("dc", p), lambda: pair_wait(dcol, dcr, p, OWN), use)
-
-    def row_points(r):
-        def use():
-            for s in (2 * r, 2 * r + 1):
-                fa[r, (s - 2 * r) * CH : (s - 2 * r + 1) * CH, :] = features(drow[s] / scales * SCALE, True).T.astype(BF16)
-
-        need(("dr", r), lambda: pair_wait(drow, drr, r, 0), use)
-
-    def vectors(key, buf, sem, pair, own, out):
-        def use():
-            for s in (2 * pair, 2 * pair + 1):
-                out[pair, :, (s - 2 * pair) * CH : (s - 2 * pair + 1) * CH] = split32(buf[s])
-
-        need((key, pair), lambda: pair_wait(buf, sem, pair, own), use)
+
+    def column_chunks(p):
+        pair_wait(dcol, dcr, p, OWN)
+        pair_wait(tcol, tcr, p, OWN)
+
+    def row_chunks(r):
+        pair_wait(drow, drr, r, 0)
+        pair_wait(trow, trr, r, 0)
+
+    def column_inputs(p):
+        for h in (0, 1):
+            fb[p, :, h * CH : (h + 1) * CH] = features(dcol[2 * p + h] / scales * SCALE, False).astype(BF16)
+
+    def row_inputs(r):
+        for h in (0, 1):
+            fa[r, h * CH : (h + 1) * CH, :] = features(drow[2 * r + h] / scales * SCALE, True).T.astype(BF16)
+
+    def vectors(buf, pair, out):
+        for h in (0, 1):
+            out[pair, :, h * CH : (h + 1) * CH] = split32(buf[2 * pair + h])
+
+    place = {job: i for i, job in enumerate(JOBS)}
+
+    def held(r, p):
+        i = place[r, p]
+        return (ka, kb)[i % 2].at[i // 2], (la, lb)[i % 2].at[i // 2]
 
     def tile(r, p):
-        for q in range(0, TILE, SUB):
-            k = kernel_values(dot(fa[r, q : q + SUB, :], fb[p], 1, 0))
-            hi = k.astype(BF16)
-            khi[r, p, q : q + SUB, :] = hi
-            klo[r, p, q : q + SUB, :] = (k - hi.astype(F32)).astype(BF16)
+        k = kernel_values(dot(fa[r], fb[p], 1, 0))
+        high, low = held(r, p)
+        hi = k.astype(BF16)
+        high[...] = hi
+        low[...] = (k - hi.astype(F32)).astype(BF16)
 
     def to_rows(r, p):
-        yrow[r] += folded(dot(vc[p], khi[r, p], 1, 1)) + dot(vc[p, 0:NRHS], klo[r, p], 1, 1)
+        high, low = held(r, p)
+        yrow[r] += folded(dot(vc[p], high[...], 1, 1)) + dot(vc[p, 0:NRHS], low[...], 1, 1)
 
     def to_cols(r, p):
         if r > 1 or p not in ONE_WAY:
-            ycol[p] += folded(dot(vr[r], khi[r, p], 1, 0)) + dot(vr[r, 0:NRHS], klo[r, p], 1, 0)
+            high, low = held(r, p)
+            ycol[p] += folded(dot(vr[r], high[...], 1, 0)) + dot(vr[r, 0:NRHS], low[...], 1, 0)
 
     def send_row(k, r):
         for s in (2 * r, 2 * r + 1):
@@ -222,32 +228,35 @@
             own += rxc[k, i]
         return own * QUAD
 
-    jobs = [(0, p) for p in (4, 3, 2, 1, 0)] + [(1, p) for p in (0, 1, 2, 3, 4)] + [(4, p) for p in range(8)]
-    col_last = (0, 7, 1, 6, 2, 5, 3, 4)
-    jobs += [(r, p) for p in col_last for r in (3, 2)]
-    lag = 3
-    for i in range(len(jobs) + lag):
-        if i < len(jobs):
-            r, p = jobs[i]
-            row_points(r)
-            col_points(p)
-            tile(r, p)
-        if i >= lag:
-            r, p = jobs[i - lag]
-            vectors("tc", tcol, tcr, p, OWN, vc)
-            vectors("tr", trow, trr, r, 0, vr)
-            to_rows(r, p)
-            to_cols(r, p)
-            if i - lag == 4:
-                send_row(0, 0)
-            if i - lag == 9:
-                send_row(0, 1)
-            if i - lag == 17:
-                send_row(0, 4)
-            if i - lag >= 18 and r == 2:
-                send_col(0, p)
-    send_row(0, 3)
-    send_row(0, 2)
+    rows_left = {r: sum(job[0] == r for job in JOBS) for r in range(NR // 2)}
+    cols_left = {p: sum(job[1] == p for job in JOBS) for p in range(NC // 2)}
+    done = 0
+    for stage, (rows, cols, upto) in enumerate(STAGES):
+        for r in rows:
+            row_chunks(r)
+        for p in cols:
+            column_chunks(p)
+        for r in rows:
+            row_inputs(r)
+            vectors(trow, r, vr)
+        for p in cols:
+            column_inputs(p)
+            vectors(tcol, p, vc)
+        last = stage == len(STAGES) - 1
+        start = 0 if stage == 0 else STAGES[stage - 1][2]
+        for i in range(start, upto + (LAG if last else 0)):
+            if i < upto:
+                tile(*JOBS[i])
+            if i >= LAG:
+                r, p = JOBS[i - LAG]
+                to_rows(r, p)
+                to_cols(r, p)
+                rows_left[r] -= 1
+                cols_left[p] -= 1
+                if cols_left[p] == 0:
+                    send_col(0, p)
+                if rows_left[r] == 0:
+                    send_row(0, r)
 
     sent(dcol.at[0 : NC - 1], 0)
     sent(drow.at[0 : NR - 1], 1)
@@ -261,7 +270,7 @@
 
     fcol[OWN] = first
     frow[0] = first
-    gather(fcol.at[OWN], fcol, fcr, frow, frr, 8)
+    gather((fcol.at[OWN], fcol, fcr, frow, frr, 8))
 
     delta = jnp.sum(first * own, 1, keepdims=True)
     marked = jnp.where(lane == sub, gamma, 0.0) + jnp.where(lane == sub + NRHS, delta, 0.0)
@@ -272,29 +281,46 @@
     yrow[...] = jnp.zeros_like(yrow)
     ycol[...] = jnp.zeros_like(ycol)
 
+    def second(rows, cols):
+        for r in rows:
+            pair_wait(frow, frr, r, 0)
+        for p in cols:
+            pair_wait(fcol, fcr, p, OWN)
+        for r in rows:
+            vectors(frow, r, vr)
+        for p in cols:
+            vectors(fcol, p, vc)
+
     def from_row(r):
-        vectors("fr", frow, frr, r, 0, vr)
         for p in HALF if r < 2 else range(8):
             to_cols(r, p)
 
     def from_col(p):
-        vectors("fc", fcol, fcr, p, OWN, vc)
         for r in range(5) if p in HALF else (2, 3, 4):
             to_rows(r, p)
 
+    second((0, 2), (4, 5))
+    from_col(4)
     from_row(0)
-    from_col(4)
     from_col(5)
     from_row(2)
+    second((3,), (3, 2, 6))
     from_col(3)
     from_col(2)
     from_col(6)
     from_row(3)
+    second((1, 4), (0, 1, 7))
+    from_col(0)
     from_col(1)
     from_col(7)
-    from_col(0)
     for r in (1, 4, 3, 2, 0):
         send_row(1, r)
+    from_row(4)
+    for p in (0, 7, 6, 3, 5):
+        send_col(1, p)
+    from_row(1)
+    for p in (1, 2, 4):
+        send_col(1, p)
     remote(stats, stats, 0, sts.at[0], col_peer(0, 1)).wait_recv()
     group = mine[0]
     for i in range(NC - 1):
@@ -302,12 +328,6 @@
     mine[1] = group
     for i, o in enumerate(ROW_PEERS):
         remote(mine.at[1], tot.at[i], 11, sts.at[1], row_at(*o)).start()
-    from_row(4)
-    for p in (0, 7, 6, 3, 5):
-        send_col(1, p)
-    from_row(1)
-    for p in (1, 2, 4):
-        send_col(1, p)
 
     sent(txr.at[0], 4)
     sent(txc.at[0], 5)
@@ -347,7 +367,7 @@
             chunks(2, NR - 1, NRHS), chunks(2, NC - 1, NRHS), chunks(2, NR - 1, NRHS), chunks(2, NC - 1, NRHS),
             pltpu.VMEM((NR // 2, TILE, 64), BF16), pltpu.VMEM((NC // 2, 64, TILE), BF16),
             pltpu.VMEM((NC // 2, 2 * NRHS, TILE), BF16), pltpu.VMEM((NR // 2, 2 * NRHS, TILE), BF16),
-            pltpu.VMEM((NR // 2, NC // 2, TILE, TILE), BF16), pltpu.VMEM((NR // 2, NC // 2, TILE, TILE), BF16),
+            *[pltpu.VMEM((len(JOBS) // 2, TILE, TILE), BF16)] * 4,
             pltpu.VMEM((NR // 2, NRHS, TILE), F32), pltpu.VMEM((NC // 2, NRHS, TILE), F32),
             dma((7,)), dma((12,)), dma((NC // 2,)), dma((NR // 2,)), dma((NC // 2,)), dma((NR // 2,)),
             dma((NC // 2,)), dma((NR // 2,)), dma((2, 2)), dma((2,)),

time: 48.4 us -> 42.7 us (0.88)
  Pallas kernels: 45.6 us -> 39.9 us
    pallas_call x1, Pallas kernels: 45.6 us -> 39.9 us  [on_device(): pl.pallas_call(cg_kernel, out_shape=(out, out, out), in_specs=[hbm] * 5,...]
where the time goes in v3:
time: 42.7 us; the launch traced here: 42.6 us
  Pallas kernels  39.9 us (93%)
  other arithmetic  1.34 us (3%)
  between operations  1.3 us (3%)
    pallas_call x1, Pallas kernels, on_device(): pl.pallas_call(cg_kernel, out_shape=(out, out, out), in_specs=[hbm] * 5,...  39.9 us
    sub x1, other arithmetic, on_device(): first - alphas * further  1.34 us

profile of v3, /device:TPU:1, one launch (start us, length us, event | category | flops | bytes accessed | tf_op | source)
XLA Modules:
  0.0 42.6 jit_solution(10206671477420244919)
XLA Ops:
  1.3 0.0 copy-start
  1.3 39.9 %shard_map.76 = (f32[16,128]{1,0:T(8,128)}, f32[16,128]{1,0:T(8,128)}, f32[16,128]{1,0:T(8,128)}) custom-call(f32[8,128]{1,0:T(8,128)} %design_ref.1, f32[8]{0:T(128)} %scales_ref.1, s32[1,128]{1,0:T(1,128)} %bitcast.1, f32[1]{0:T(128)S(6)} %copy.8.noise_ref, f32[16,128]{1,0:T(8,128)} %targets_ref.1), custom_call_target="tpu_custom_call" | custom-call | tf_op jit(solution)/shard_map/pallas_call | solution.py:358
  41.2 0.0 copy-done
  41.2 1.3 %multiply_subtract_fusion = (f32[16,128]{1,0:T(8,128)}, f32[16,128]{1,0:T(8,128)}, f32[16,128]{1,0:T(8,128)}) fusion(f32[16,128]{1,0:T(8,128)} %get-tuple-element.7, f32[16,128]{1,0:T(8,128)} %get-tuple-element.6, f32[16,128]{1,0:T(8,128)} %get-tuple-element.8, f32[16,128]{1,0:T(8,128)S(1)} %copy-done), kind=kLoop, calls=%fused_computation | loop fusion | flops 10240 | bytes 57344 | tf_op jit(solution)/shard_map/sub | solution.py:377
Async XLA Ops:
  1.3 39.9 %copy-start = (f32[16,128]{1,0:T(8,128)S(1)}, f32[16,128]{1,0:T(8,128)}, u32[]{:S(2)}) copy-start(f32[16,128]{1,0:T(8,128)} %targets_ref.1) | copy-start | bytes 24580

commit v4 on v3

--- a/solution.py
+++ b/solution.py
@@ -23,13 +23,19 @@
 NC, NR = len(COLS), len(ROWS)
 OWN = COLS.index((0, 0))
 TILE = 2 * CH
-LAG = 3
-JOBS = (
-    (0, 4), (0, 3), (0, 2), (2, 2), (2, 6), (3, 4), (3, 5), (3, 3), (3, 2), (3, 6),
-    (1, 0), (1, 1), (1, 2), (1, 3), (1, 4), (4, 0), (0, 0), (2, 0), (3, 0), (4, 7), (2, 7), (3, 7),
-    (4, 1), (0, 1), (2, 1), (3, 1), (4, 2), (4, 6), (4, 3), (4, 4), (4, 5), (2, 3), (2, 4), (2, 5),
+BLOCKS = (
+    ((0, 2, 3), (4, 5, 3, 2, 6), ((0, 4), (3, 4), (3, 5), (0, 3), (3, 3)), ()),
+    ((), (), ((3, 2), (0, 2), (2, 2), (2, 6), (3, 6)), ((3, 4), (3, 5), (3, 3))),
+    ((), (), ((2, 3), (2, 4), (2, 5)), ((3, 2), (0, 2), (2, 2), (2, 6), (3, 6))),
+    ((1, 4), (0, 1, 7), ((1, 0), (1, 1), (1, 2), (1, 3), (1, 4)), ((2, 3),)),
+    ((), (), ((4, 0), (0, 0), (2, 0), (3, 0), (4, 7)), ((1, 0), (1, 1), (1, 2), (1, 3), (1, 4))),
+    ((), (), ((2, 7), (3, 7), (4, 1), (0, 1), (2, 1), (3, 1)), ((4, 0), (0, 0), (2, 0), (3, 0), (4, 7))),
+    ((), (), ((4, 2), (4, 6), (4, 3), (4, 4), (4, 5)), ((2, 7), (3, 7), (4, 1), (0, 1), (2, 1), (3, 1))),
+    ((), (), (), ((4, 2), (4, 6), (4, 3), (4, 4), (4, 5))),
+    ((), (), (), ((0, 4), (0, 3), (2, 4), (2, 5))),
 )
-STAGES = (((0, 2, 3), (4, 5, 3, 2, 6), 10), ((1, 4), (0, 1, 7), len(JOBS)))
+JOBS = tuple(job for block in BLOCKS for job in block[2])
+assert len(set(JOBS)) == 34 and sorted(JOBS) == sorted(job for block in BLOCKS for job in block[3])
 HALF = (0, 1, 2, 3, 4)
 ONE_WAY = (0, 3)
 ROW_PEERS = tuple(sorted(((dz, dc) for dz in range(8) for dc in range(2) if dz or dc), key=lambda o: -min(o[0], 8 - o[0])))
@@ -113,10 +119,10 @@
         return row_at(sign * ROWS[slot][0], ROWS[slot][1])
 
     barrier = pltpu.get_barrier_semaphore()
-    for s in COL_ORDER:
-        pl.semaphore_signal(barrier, inc=1, device_id=col_peer(s, 1), device_id_type=MESH)
-    for o in ROW_PEERS:
-        pl.semaphore_signal(barrier, inc=1, device_id=row_at(*o), device_id_type=MESH)
+    peers = [(hops(COLS[s], (4, 4)), col_peer(s, 1)) for s in COL_ORDER]
+    peers += [(min(o[0], 8 - o[0]), row_at(*o)) for o in ROW_PEERS]
+    for _, peer in sorted(peers, key=lambda o: -o[0]):
+        pl.semaphore_signal(barrier, inc=1, device_id=peer, device_id_type=MESH)
 
     local = [
         pltpu.make_async_copy(src, dst, lsem.at[i])
@@ -196,14 +202,26 @@
         high[...] = hi
         low[...] = (k - hi.astype(F32)).astype(BF16)
 
-    def to_rows(r, p):
-        high, low = held(r, p)
-        yrow[r] += folded(dot(vc[p], high[...], 1, 1)) + dot(vc[p, 0:NRHS], low[...], 1, 1)
-
-    def to_cols(r, p):
-        if r > 1 or p not in ONE_WAY:
-            high, low = held(r, p)
-            ycol[p] += folded(dot(vr[r], high[...], 1, 0)) + dot(vr[r, 0:NRHS], low[...], 1, 0)
+    def joined(values, axis):
+        return jnp.concatenate(values, axis) if len(values) > 1 else values[0]
+
+    def products(jobs):
+        jobs = [(is_col, own, [o for o in over if not is_col or o > 1 or own not in ONE_WAY]) for is_col, own, over in jobs]
+        jobs = [job for job in jobs if job[2]]
+        operands = []
+        for is_col, own, over in jobs:
+            vectors_of = (vc, vr)[is_col]
+            high, low = ([t[...] for t in tiles] for tiles in zip(*(held(*((o, own) if is_col else (own, o))) for o in over)))
+            operands.append((joined([vectors_of[o] for o in over], 1), joined(high, 1 - is_col), joined(low, 1 - is_col)))
+        first = [folded(dot(v, hi, 1, 1 - job[0])) for job, (v, hi, _) in zip(jobs, operands)]
+        second = [dot(v[0:NRHS], lo, 1, 1 - job[0]) for job, (v, _, lo) in zip(jobs, operands)]
+        for (is_col, own, _), a, b in zip(jobs, first, second):
+            (yrow, ycol)[is_col][own] += a + b
+
+    def apart(jobs):
+        @pl.when(blk >= 0)
+        def _():
+            products(jobs)
 
     def send_row(k, r):
         for s in (2 * r, 2 * r + 1):
@@ -230,33 +248,39 @@
 
     rows_left = {r: sum(job[0] == r for job in JOBS) for r in range(NR // 2)}
     cols_left = {p: sum(job[1] == p for job in JOBS) for p in range(NC // 2)}
-    done = 0
-    for stage, (rows, cols, upto) in enumerate(STAGES):
+    for rows, cols, values, sums in BLOCKS:
         for r in rows:
             row_chunks(r)
         for p in cols:
             column_chunks(p)
-        for r in rows:
-            row_inputs(r)
-            vectors(trow, r, vr)
-        for p in cols:
-            column_inputs(p)
-            vectors(tcol, p, vc)
-        last = stage == len(STAGES) - 1
-        start = 0 if stage == 0 else STAGES[stage - 1][2]
-        for i in range(start, upto + (LAG if last else 0)):
-            if i < upto:
-                tile(*JOBS[i])
-            if i >= LAG:
-                r, p = JOBS[i - LAG]
-                to_rows(r, p)
-                to_cols(r, p)
-                rows_left[r] -= 1
-                cols_left[p] -= 1
-                if cols_left[p] == 0:
-                    send_col(0, p)
-                if rows_left[r] == 0:
-                    send_row(0, r)
+
+        @pl.when(blk >= 0)
+        def _(rows=rows, cols=cols, values=values, sums=sums):
+            for r in rows:
+                row_inputs(r)
+                vectors(trow, r, vr)
+            for p in cols:
+                column_inputs(p)
+                vectors(tcol, p, vc)
+            for i in range(max(len(values), len(sums))):
+                if i < len(values):
+                    tile(*values[i])
+                if i < len(sums):
+                    r, p = sums[i]
+                    products([(0, r, (p,))])
+                    products([(1, p, (r,))])
+
+        for r, p in sums:
+            rows_left[r] -= 1
+            cols_left[p] -= 1
+        for r in range(NR // 2):
+            if rows_left[r] == 0:
+                rows_left[r] = -1
+                send_row(0, r)
+        for p in range(NC // 2):
+            if cols_left[p] == 0:
+                cols_left[p] = -1
+                send_col(0, p)
 
     sent(dcol.at[0 : NC - 1], 0)
     sent(drow.at[0 : NR - 1], 1)
@@ -291,36 +315,23 @@
         for p in cols:
             vectors(fcol, p, vc)
 
-    def from_row(r):
-        for p in HALF if r < 2 else range(8):
-            to_cols(r, p)
-
-    def from_col(p):
-        for r in range(5) if p in HALF else (2, 3, 4):
-            to_rows(r, p)
-
-    second((0, 2), (4, 5))
-    from_col(4)
-    from_row(0)
-    from_col(5)
-    from_row(2)
-    second((3,), (3, 2, 6))
-    from_col(3)
-    from_col(2)
-    from_col(6)
-    from_row(3)
-    second((1, 4), (0, 1, 7))
-    from_col(0)
-    from_col(1)
-    from_col(7)
-    for r in (1, 4, 3, 2, 0):
+    near, far = ((0, 2, 3), (4, 5, 3, 2, 6)), ((1, 4), (0, 1, 7))
+
+    def met(is_col, own, others):
+        return tuple(o for o in others if ((o if is_col else own) > 1 or (own if is_col else o) in HALF))
+
+    second(near[0], near[1])
+    apart([(0, r, met(0, r, near[1])) for r in (1, 4, 3, 2, 0)])
+    apart([(1, p, met(1, p, near[0])) for p in (0, 7, 1, 2, 6, 3, 4, 5)])
+    second(far[0], far[1])
+    apart([(0, r, met(0, r, far[1])) for r in (1, 4)])
+    send_row(1, 1)
+    send_row(1, 4)
+    apart([(1, p, met(1, p, far[0])) for p in (0, 7, 1)] + [(0, r, met(0, r, far[1])) for r in (3, 2, 0)])
+    for p in (0, 7, 1):
+        send_col(1, p)
+    for r in (3, 2, 0):
         send_row(1, r)
-    from_row(4)
-    for p in (0, 7, 6, 3, 5):
-        send_col(1, p)
-    from_row(1)
-    for p in (1, 2, 4):
-        send_col(1, p)
     remote(stats, stats, 0, sts.at[0], col_peer(0, 1)).wait_recv()
     group = mine[0]
     for i in range(NC - 1):
@@ -328,6 +339,9 @@
     mine[1] = group
     for i, o in enumerate(ROW_PEERS):
         remote(mine.at[1], tot.at[i], 11, sts.at[1], row_at(*o)).start()
+    apart([(1, p, met(1, p, far[0])) for p in (2, 6, 3, 4, 5)])
+    for p in (2, 6, 3, 4, 5):
+        send_col(1, p)
 
     sent(txr.at[0], 4)
     sent(txc.at[0], 5)
@@ -351,6 +365,9 @@
     out = jax.ShapeDtypeStruct((NRHS, CH), F32)
     vmem, hbm = (pl.BlockSpec(memory_space=m) for m in (pltpu.VMEM, pltpu.HBM))
     dma = pltpu.SemaphoreType.DMA
+
+    def in_hbm(a):
+        return pltpu.with_memory_space_constraint(a, pltpu.HBM)
 
     def chunks(*shape):
         return pltpu.VMEM(shape + (CH,), F32)
@@ -372,8 +389,8 @@
             dma((7,)), dma((12,)), dma((NC // 2,)), dma((NR // 2,)), dma((NC // 2,)), dma((NR // 2,)),
             dma((NC // 2,)), dma((NR // 2,)), dma((2, 2)), dma((2,)),
         ],
-        compiler_params=pltpu.CompilerParams(collective_id=0, has_side_effects=True),
-    )(design, lengthscales, counts.reshape(1, CH), noise_base, targets)
+        compiler_params=pltpu.CompilerParams(collective_id=0, has_side_effects=True, vmem_limit_bytes=48 << 20),
+    )(in_hbm(design), in_hbm(lengthscales), in_hbm(counts.reshape(1, CH)), noise_base, in_hbm(targets))
     return alphas * targets, targets - alphas * first, first - alphas * further
 
 

time: 42.7 us -> 41.5 us (0.972)
  other arithmetic: 1.34 us -> 0.61 us
    sub x1, other arithmetic: 1.34 us -> 0.61 us  [on_device(): first - alphas * further]
    pallas_call x1, Pallas kernels: 39.9 us -> 39.5 us  [on_device(): pl.pallas_call(cg_kernel, out_shape=(out, out, out), in_specs=[hbm] * 5,...]
where the time goes in v4:
time: 41.5 us; the launch traced here: 41.4 us
  Pallas kernels  39.5 us (95%)
  between operations  1.3 us (3%)
  other arithmetic  0.61 us (1%)
    pallas_call x1, Pallas kernels, on_device(): pl.pallas_call(cg_kernel, out_shape=(out, out, out), in_specs=[hbm] * 5,...  39.5 us

profile of v4, /device:TPU:1, one launch (start us, length us, event | category | flops | bytes accessed | tf_op | source)
XLA Modules:
  0.0 41.4 jit_solution(3517270883906944770)
XLA Ops:
  1.3 0.0 copy-start
  1.3 39.5 %shard_map.76 = (f32[16,128]{1,0:T(8,128)S(1)}, f32[16,128]{1,0:T(8,128)S(1)}, f32[16,128]{1,0:T(8,128)S(1)}) custom-call(f32[8,128]{1,0:T(8,128)} %design_ref.1, f32[8]{0:T(128)} %scales_ref.1, s32[1,128]{1,0:T(1,128)} %bitcast.1, f32[1]{0:T(128)S(6)} %copy.8.noise_ref, f32[16,128]{1,0:T(8,128)} %targets_ref.1), custom_call_target="tpu_custom_call" | custom-call | tf_op jit(solution)/shard_map/pallas_call | solution.py:375
  40.8 0.0 copy-done
  40.8 0.6 %multiply_subtract_fusion = (f32[16,128]{1,0:T(8,128)}, f32[16,128]{1,0:T(8,128)}, f32[16,128]{1,0:T(8,128)}) fusion(f32[16,128]{1,0:T(8,128)S(1)} %get-tuple-element.7, f32[16,128]{1,0:T(8,128)S(1)} %get-tuple-element.6, f32[16,128]{1,0:T(8,128)S(1)} %get-tuple-element.8, f32[16,128]{1,0:T(8,128)S(1)} %copy-done), kind=kLoop, calls=%fused_computation | loop fusion | flops 10240 | bytes 57344 | tf_op jit(solution)/shard_map/sub | solution.py:394
Async XLA Ops:
  1.3 39.5 %copy-start = (f32[16,128]{1,0:T(8,128)S(1)}, f32[16,128]{1,0:T(8,128)}, u32[]{:S(2)}) copy-start(f32[16,128]{1,0:T(8,128)} %targets_ref.1) | copy-start | bytes 24580

commit v5 on v4

--- a/solution.py
+++ b/solution.py
@@ -23,16 +23,16 @@
 NC, NR = len(COLS), len(ROWS)
 OWN = COLS.index((0, 0))
 TILE = 2 * CH
+NEAR, FAR, NONE = ((0, 2, 3), (4, 5, 3, 2, 6)), ((1, 4), (0, 1, 7)), ((), ())
 BLOCKS = (
-    ((0, 2, 3), (4, 5, 3, 2, 6), ((0, 4), (3, 4), (3, 5), (0, 3), (3, 3)), ()),
-    ((), (), ((3, 2), (0, 2), (2, 2), (2, 6), (3, 6)), ((3, 4), (3, 5), (3, 3))),
-    ((), (), ((2, 3), (2, 4), (2, 5)), ((3, 2), (0, 2), (2, 2), (2, 6), (3, 6))),
-    ((1, 4), (0, 1, 7), ((1, 0), (1, 1), (1, 2), (1, 3), (1, 4)), ((2, 3),)),
-    ((), (), ((4, 0), (0, 0), (2, 0), (3, 0), (4, 7)), ((1, 0), (1, 1), (1, 2), (1, 3), (1, 4))),
-    ((), (), ((2, 7), (3, 7), (4, 1), (0, 1), (2, 1), (3, 1)), ((4, 0), (0, 0), (2, 0), (3, 0), (4, 7))),
-    ((), (), ((4, 2), (4, 6), (4, 3), (4, 4), (4, 5)), ((2, 7), (3, 7), (4, 1), (0, 1), (2, 1), (3, 1))),
-    ((), (), (), ((4, 2), (4, 6), (4, 3), (4, 4), (4, 5))),
-    ((), (), (), ((0, 4), (0, 3), (2, 4), (2, 5))),
+    (NEAR, NONE, ((3, 4), (3, 5), (3, 3), (3, 2), (0, 2)), ()),
+    (NONE, NEAR, ((2, 2), (2, 6), (3, 6), (0, 4), (0, 3)), ((3, 4), (3, 5), (3, 3), (3, 2), (0, 2))),
+    (FAR, NONE, ((1, 0), (1, 1), (1, 2), (1, 3), (1, 4)), ((2, 2), (2, 6), (3, 6))),
+    (NONE, FAR, ((4, 0), (0, 0), (2, 0), (3, 0), (4, 7), (2, 7)), ((1, 0), (1, 1), (1, 2), (1, 3), (1, 4))),
+    (NONE, NONE, ((3, 7), (4, 1), (0, 1), (2, 1), (3, 1)), ((4, 0), (0, 0), (2, 0), (3, 0), (4, 7), (2, 7))),
+    (NONE, NONE, ((4, 2), (4, 6), (4, 3), (4, 4), (4, 5)), ((3, 7), (4, 1), (0, 1), (2, 1), (3, 1))),
+    (NONE, NONE, ((2, 3), (2, 4), (2, 5)), ((4, 2), (4, 6), (4, 3), (4, 4), (4, 5))),
+    (NONE, NONE, (), ((0, 4), (0, 3), (2, 3), (2, 4), (2, 5))),
 )
 JOBS = tuple(job for block in BLOCKS for job in block[2])
 assert len(set(JOBS)) == 34 and sorted(JOBS) == sorted(job for block in BLOCKS for job in block[3])
@@ -157,7 +157,8 @@
     def sent(ref, at):
         remote(ref, ref, at, rxs.at[0, 0], col_peer(0, 1)).wait_send()
 
-    gather((design_ref, dcol, dcr, drow, drr, 0), (targets_ref, tcol, tcr, trow, trr, 2))
+    gather((design_ref, dcol, dcr, drow, drr, 0))
+    gather((targets_ref, tcol, tcr, trow, trr, 2))
 
     for c in local:
         c.wait()
@@ -168,14 +169,6 @@
     noise = noise_sm[0] / counts_vm[...].astype(F32)
     yrow[...] = jnp.zeros_like(yrow)
     ycol[...] = jnp.zeros_like(ycol)
-
-    def column_chunks(p):
-        pair_wait(dcol, dcr, p, OWN)
-        pair_wait(tcol, tcr, p, OWN)
-
-    def row_chunks(r):
-        pair_wait(drow, drr, r, 0)
-        pair_wait(trow, trr, r, 0)
 
     def column_inputs(p):
         for h in (0, 1):
@@ -248,19 +241,25 @@
 
     rows_left = {r: sum(job[0] == r for job in JOBS) for r in range(NR // 2)}
     cols_left = {p: sum(job[1] == p for job in JOBS) for p in range(NC // 2)}
-    for rows, cols, values, sums in BLOCKS:
-        for r in rows:
-            row_chunks(r)
-        for p in cols:
-            column_chunks(p)
+    for points, targets, values, sums in BLOCKS:
+        for r in points[0]:
+            pair_wait(drow, drr, r, 0)
+        for p in points[1]:
+            pair_wait(dcol, dcr, p, OWN)
+        for r in targets[0]:
+            pair_wait(trow, trr, r, 0)
+        for p in targets[1]:
+            pair_wait(tcol, tcr, p, OWN)
 
         @pl.when(blk >= 0)
-        def _(rows=rows, cols=cols, values=values, sums=sums):
-            for r in rows:
+        def _(points=points, targets=targets, values=values, sums=sums):
+            for r in points[0]:
                 row_inputs(r)
+            for p in points[1]:
+                column_inputs(p)
+            for r in targets[0]:
                 vectors(trow, r, vr)
-            for p in cols:
-                column_inputs(p)
+            for p in targets[1]:
                 vectors(tcol, p, vc)
             for i in range(max(len(values), len(sums))):
                 if i < len(values):
@@ -315,23 +314,18 @@
         for p in cols:
             vectors(fcol, p, vc)
 
-    near, far = ((0, 2, 3), (4, 5, 3, 2, 6)), ((1, 4), (0, 1, 7))
-
     def met(is_col, own, others):
         return tuple(o for o in others if ((o if is_col else own) > 1 or (own if is_col else o) in HALF))
 
-    second(near[0], near[1])
-    apart([(0, r, met(0, r, near[1])) for r in (1, 4, 3, 2, 0)])
-    apart([(1, p, met(1, p, near[0])) for p in (0, 7, 1, 2, 6, 3, 4, 5)])
-    second(far[0], far[1])
-    apart([(0, r, met(0, r, far[1])) for r in (1, 4)])
+    second(NEAR[0], NEAR[1])
+    apart([(0, r, met(0, r, NEAR[1])) for r in (1, 4)] + [(1, p, met(1, p, NEAR[0])) for p in (0, 7, 1)])
+    second(FAR[0], FAR[1])
+    apart([(0, r, met(0, r, FAR[1])) for r in (1, 4)])
     send_row(1, 1)
     send_row(1, 4)
-    apart([(1, p, met(1, p, far[0])) for p in (0, 7, 1)] + [(0, r, met(0, r, far[1])) for r in (3, 2, 0)])
+    apart([(1, p, met(1, p, FAR[0])) for p in (0, 7, 1)])
     for p in (0, 7, 1):
         send_col(1, p)
-    for r in (3, 2, 0):
-        send_row(1, r)
     remote(stats, stats, 0, sts.at[0], col_peer(0, 1)).wait_recv()
     group = mine[0]
     for i in range(NC - 1):
@@ -339,9 +333,13 @@
     mine[1] = group
     for i, o in enumerate(ROW_PEERS):
         remote(mine.at[1], tot.at[i], 11, sts.at[1], row_at(*o)).start()
-    apart([(1, p, met(1, p, far[0])) for p in (2, 6, 3, 4, 5)])
+    apart([(0, r, met(0, r, range(NC // 2))) for r in (3, 2)])
+    send_row(1, 3)
+    send_row(1, 2)
+    apart([(1, p, met(1, p, range(NR // 2))) for p in (2, 6, 3, 4, 5)] + [(0, 0, HALF)])
     for p in (2, 6, 3, 4, 5):
         send_col(1, p)
+    send_row(1, 0)
 
     sent(txr.at[0], 4)
     sent(txc.at[0], 5)

time: 41.5 us -> 40.1 us (0.966)
  Pallas kernels: 39.5 us -> 38 us
    pallas_call x1, Pallas kernels: 39.5 us -> 38 us  [on_device(): pl.pallas_call(cg_kernel, out_shape=(out, out, out), in_specs=[hbm] * 5,...]
where the time goes in v5:
time: 40.1 us; the launch traced here: 40 us
  Pallas kernels  38 us (95%)
  between operations  1.3 us (3%)
  other arithmetic  0.61 us (2%)
    pallas_call x1, Pallas kernels, on_device(): pl.pallas_call(cg_kernel, out_shape=(out, out, out), in_specs=[hbm] * 5,...  38 us

profile of v5, /device:TPU:1, one launch (start us, length us, event | category | flops | bytes accessed | tf_op | source)
XLA Modules:
  0.0 40.0 jit_solution(931535819014060599)
XLA Ops:
  1.3 0.0 copy-start
  1.3 38.0 %shard_map.76 = (f32[16,128]{1,0:T(8,128)S(1)}, f32[16,128]{1,0:T(8,128)S(1)}, f32[16,128]{1,0:T(8,128)S(1)}) custom-call(f32[8,128]{1,0:T(8,128)} %design_ref.1, f32[8]{0:T(128)} %scales_ref.1, s32[1,128]{1,0:T(1,128)} %bitcast.1, f32[1]{0:T(128)S(6)} %copy.8.noise_ref, f32[16,128]{1,0:T(8,128)} %targets_ref.1), custom_call_target="tpu_custom_call" | custom-call | tf_op jit(solution)/shard_map/pallas_call | solution.py:373
  39.3 0.0 copy-done
  39.4 0.6 %multiply_subtract_fusion = (f32[16,128]{1,0:T(8,128)}, f32[16,128]{1,0:T(8,128)}, f32[16,128]{1,0:T(8,128)}) fusion(f32[16,128]{1,0:T(8,128)S(1)} %get-tuple-element.7, f32[16,128]{1,0:T(8,128)S(1)} %get-tuple-element.6, f32[16,128]{1,0:T(8,128)S(1)} %get-tuple-element.8, f32[16,128]{1,0:T(8,128)S(1)} %copy-done), kind=kLoop, calls=%fused_computation | loop fusion | flops 10240 | bytes 57344 | tf_op jit(solution)/shard_map/sub | solution.py:392
Async XLA Ops:
  1.3 38.1 %copy-start = (f32[16,128]{1,0:T(8,128)S(1)}, f32[16,128]{1,0:T(8,128)}, u32[]{:S(2)}) copy-start(f32[16,128]{1,0:T(8,128)} %targets_ref.1) | copy-start | bytes 24580

commit v6 on v5

--- a/solution.py
+++ b/solution.py
@@ -93,7 +93,7 @@
     scales_sm, noise_sm, counts_vm,
     dcol, drow, tcol, trow, fcol, frow, stats, tot, mine,
     txr, txc, rxr, rxc,
-    fa, fb, vc, vr, ka, kb, la, lb, yrow, ycol,
+    fa, fb, vc, vr, ka, kb, la, lb, kt, lt, yrow, ycol,
     lsem, ssem, dcr, drr, tcr, trr, fcr, frr, rxs, sts,
 ):
     blk, grp = lax.axis_index("blk"), lax.axis_index("grp")
@@ -198,23 +198,34 @@
     def joined(values, axis):
         return jnp.concatenate(values, axis) if len(values) > 1 else values[0]
 
-    def products(jobs):
+    def turn(jobs):
+        @pl.when(blk >= 0)
+        def _():
+            for job in jobs:
+                for of, to in zip(held(*job), (kt, lt)):
+                    to[place[job]] = of[...].T
+
+    def products(jobs, turned=False):
         jobs = [(is_col, own, [o for o in over if not is_col or o > 1 or own not in ONE_WAY]) for is_col, own, over in jobs]
         jobs = [job for job in jobs if job[2]]
         operands = []
         for is_col, own, over in jobs:
             vectors_of = (vc, vr)[is_col]
-            high, low = ([t[...] for t in tiles] for tiles in zip(*(held(*((o, own) if is_col else (own, o))) for o in over)))
-            operands.append((joined([vectors_of[o] for o in over], 1), joined(high, 1 - is_col), joined(low, 1 - is_col)))
-        first = [folded(dot(v, hi, 1, 1 - job[0])) for job, (v, hi, _) in zip(jobs, operands)]
-        second = [dot(v[0:NRHS], lo, 1, 1 - job[0]) for job, (v, _, lo) in zip(jobs, operands)]
+            at = 0 if is_col or turned else 1
+            if turned and not is_col:
+                high, low = ([t[place[own, o]] for o in over] for t in (kt, lt))
+            else:
+                high, low = ([t[...] for t in tiles] for tiles in zip(*(held(*((o, own) if is_col else (own, o))) for o in over)))
+            operands.append((joined([vectors_of[o] for o in over], 1), joined(high, at), joined(low, at), at))
+        first = [folded(dot(v, hi, 1, at)) for v, hi, _, at in operands]
+        second = [dot(v[0:NRHS], lo, 1, at) for v, _, lo, at in operands]
         for (is_col, own, _), a, b in zip(jobs, first, second):
             (yrow, ycol)[is_col][own] += a + b
 
     def apart(jobs):
         @pl.when(blk >= 0)
         def _():
-            products(jobs)
+            products(jobs, True)
 
     def send_row(k, r):
         for s in (2 * r, 2 * r + 1):
@@ -281,6 +292,7 @@
                 cols_left[p] = -1
                 send_col(0, p)
 
+    turn(JOBS[0:20])
     sent(dcol.at[0 : NC - 1], 0)
     sent(drow.at[0 : NR - 1], 1)
     sent(tcol.at[0 : NC - 1], 2)
@@ -303,6 +315,8 @@
     first_ref[...] = first
     yrow[...] = jnp.zeros_like(yrow)
     ycol[...] = jnp.zeros_like(ycol)
+
+    turn(JOBS[20:])
 
     def second(rows, cols):
         for r in rows:
@@ -382,7 +396,7 @@
             chunks(2, NR - 1, NRHS), chunks(2, NC - 1, NRHS), chunks(2, NR - 1, NRHS), chunks(2, NC - 1, NRHS),
             pltpu.VMEM((NR // 2, TILE, 64), BF16), pltpu.VMEM((NC // 2, 64, TILE), BF16),
             pltpu.VMEM((NC // 2, 2 * NRHS, TILE), BF16), pltpu.VMEM((NR // 2, 2 * NRHS, TILE), BF16),
-            *[pltpu.VMEM((len(JOBS) // 2, TILE, TILE), BF16)] * 4,
+            *[pltpu.VMEM((len(JOBS) // 2, TILE, TILE), BF16)] * 4, *[pltpu.VMEM((len(JOBS), TILE, TILE), BF16)] * 2,
             pltpu.VMEM((NR // 2, NRHS, TILE), F32), pltpu.VMEM((NC // 2, NRHS, TILE), F32),
             dma((7,)), dma((12,)), dma((NC // 2,)), dma((NR // 2,)), dma((NC // 2,)), dma((NR // 2,)),
             dma((NC // 2,)), dma((NR // 2,)), dma((2, 2)), dma((2,)),

time: 40.1 us -> 39.2 us (0.978)
  Pallas kernels: 38 us -> 37.2 us
    pallas_call x1, Pallas kernels: 38 us -> 37.2 us  [on_device(): pl.pallas_call(cg_kernel, out_shape=(out, out, out), in_specs=[hbm] * 5,...]
where the time goes in v6:
time: 39.2 us; the launch traced here: 39.1 us
  Pallas kernels  37.2 us (95%)
  between operations  1.3 us (3%)
  other arithmetic  0.61 us (2%)
    pallas_call x1, Pallas kernels, on_device(): pl.pallas_call(cg_kernel, out_shape=(out, out, out), in_specs=[hbm] * 5,...  37.2 us

profile of v6, /device:TPU:1, one launch (start us, length us, event | category | flops | bytes accessed | tf_op | source)
XLA Modules:
  0.0 39.1 jit_solution(15026759415706428011)
XLA Ops:
  1.3 0.0 copy-start
  1.3 37.2 %shard_map.76 = (f32[16,128]{1,0:T(8,128)S(1)}, f32[16,128]{1,0:T(8,128)S(1)}, f32[16,128]{1,0:T(8,128)S(1)}) custom-call(f32[8,128]{1,0:T(8,128)} %design_ref.1, f32[8]{0:T(128)} %scales_ref.1, s32[1,128]{1,0:T(1,128)} %bitcast.1, f32[1]{0:T(128)S(6)} %copy.8.noise_ref, f32[16,128]{1,0:T(8,128)} %targets_ref.1), custom_call_target="tpu_custom_call" | custom-call | tf_op jit(solution)/shard_map/pallas_call | solution.py:387
  38.5 0.0 copy-done
  38.5 0.6 %multiply_subtract_fusion = (f32[16,128]{1,0:T(8,128)}, f32[16,128]{1,0:T(8,128)}, f32[16,128]{1,0:T(8,128)}) fusion(f32[16,128]{1,0:T(8,128)S(1)} %get-tuple-element.7, f32[16,128]{1,0:T(8,128)S(1)} %get-tuple-element.6, f32[16,128]{1,0:T(8,128)S(1)} %get-tuple-element.8, f32[16,128]{1,0:T(8,128)S(1)} %copy-done), kind=kLoop, calls=%fused_computation | loop fusion | flops 10240 | bytes 57344 | tf_op jit(solution)/shard_map/sub | solution.py:406
Async XLA Ops:
  1.3 37.2 %copy-start = (f32[16,128]{1,0:T(8,128)S(1)}, f32[16,128]{1,0:T(8,128)}, u32[]{:S(2)}) copy-start(f32[16,128]{1,0:T(8,128)} %targets_ref.1) | copy-start | bytes 24580

commit v7 on v6

--- a/solution.py
+++ b/solution.py
@@ -272,6 +272,11 @@
                 vectors(trow, r, vr)
             for p in targets[1]:
                 vectors(tcol, p, vc)
+            if not values:
+                rows_of = {r: [q for t, q in sums if t == r] for r, _ in sums}
+                cols_of = {p: [t for t, q in sums if q == p] for _, p in sums}
+                products([(0, r, ps) for r, ps in rows_of.items()] + [(1, p, rs) for p, rs in cols_of.items()])
+                return
             for i in range(max(len(values), len(sums))):
                 if i < len(values):
                     tile(*values[i])
@@ -331,12 +336,15 @@
     def met(is_col, own, others):
         return tuple(o for o in others if ((o if is_col else own) > 1 or (own if is_col else o) in HALF))
 
-    second(NEAR[0], NEAR[1])
-    apart([(0, r, met(0, r, NEAR[1])) for r in (1, 4)] + [(1, p, met(1, p, NEAR[0])) for p in (0, 7, 1)])
-    second(FAR[0], FAR[1])
+    second((), NEAR[1])
+    apart([(0, r, met(0, r, NEAR[1])) for r in (1, 4, 3, 2)])
+    second(NEAR[0], ())
+    apart([(1, p, met(1, p, NEAR[0])) for p in (0, 7, 1)])
+    second((), FAR[1])
     apart([(0, r, met(0, r, FAR[1])) for r in (1, 4)])
     send_row(1, 1)
     send_row(1, 4)
+    second(FAR[0], ())
     apart([(1, p, met(1, p, FAR[0])) for p in (0, 7, 1)])
     for p in (0, 7, 1):
         send_col(1, p)
@@ -347,7 +355,7 @@
     mine[1] = group
     for i, o in enumerate(ROW_PEERS):
         remote(mine.at[1], tot.at[i], 11, sts.at[1], row_at(*o)).start()
-    apart([(0, r, met(0, r, range(NC // 2))) for r in (3, 2)])
+    apart([(0, r, met(0, r, FAR[1])) for r in (3, 2)])
     send_row(1, 3)
     send_row(1, 2)
     apart([(1, p, met(1, p, range(NR // 2))) for p in (2, 6, 3, 4, 5)] + [(0, 0, HALF)])

time: 39.2 us -> 39 us (level)
  no operation moved by 1% of the time
where the time goes in v7:
time: 39 us; the launch traced here: 38.9 us
  Pallas kernels  37 us (95%)
  between operations  1.3 us (3%)
  other arithmetic  0.61 us (2%)
    pallas_call x1, Pallas kernels, on_device(): pl.pallas_call(cg_kernel, out_shape=(out, out, out), in_specs=[hbm] * 5,...  37 us

profile of v7, /device:TPU:1, one launch (start us, length us, event | category | flops | bytes accessed | tf_op | source)
XLA Modules:
  0.0 38.9 jit_solution(11242911621083298707)
XLA Ops:
  1.3 0.0 copy-start
  1.3 37.0 %shard_map.76 = (f32[16,128]{1,0:T(8,128)S(1)}, f32[16,128]{1,0:T(8,128)S(1)}, f32[16,128]{1,0:T(8,128)S(1)}) custom-call(f32[8,128]{1,0:T(8,128)} %design_ref.1, f32[8]{0:T(128)} %scales_ref.1, s32[1,128]{1,0:T(1,128)} %bitcast.1, f32[1]{0:T(128)S(6)} %copy.8.noise_ref, f32[16,128]{1,0:T(8,128)} %targets_ref.1), custom_call_target="tpu_custom_call" | custom-call | tf_op jit(solution)/shard_map/pallas_call | solution.py:395
  38.3 0.0 copy-done
  38.3 0.6 %multiply_subtract_fusion = (f32[16,128]{1,0:T(8,128)}, f32[16,128]{1,0:T(8,128)}, f32[16,128]{1,0:T(8,128)}) fusion(f32[16,128]{1,0:T(8,128)S(1)} %get-tuple-element.7, f32[16,128]{1,0:T(8,128)S(1)} %get-tuple-element.6, f32[16,128]{1,0:T(8,128)S(1)} %get-tuple-element.8, f32[16,128]{1,0:T(8,128)S(1)} %copy-done), kind=kLoop, calls=%fused_computation | loop fusion | flops 10240 | bytes 57344 | tf_op jit(solution)/shard_map/sub | solution.py:414
Async XLA Ops:
  1.3 37.0 %copy-start = (f32[16,128]{1,0:T(8,128)S(1)}, f32[16,128]{1,0:T(8,128)}, u32[]{:S(2)}) copy-start(f32[16,128]{1,0:T(8,128)} %targets_ref.1) | copy-start | bytes 24580

commit v8 on v7

--- a/solution.py
+++ b/solution.py
@@ -344,6 +344,9 @@
     apart([(0, r, met(0, r, FAR[1])) for r in (1, 4)])
     send_row(1, 1)
     send_row(1, 4)
+    apart([(0, r, met(0, r, FAR[1])) for r in (3, 2)])
+    send_row(1, 3)
+    send_row(1, 2)
     second(FAR[0], ())
     apart([(1, p, met(1, p, FAR[0])) for p in (0, 7, 1)])
     for p in (0, 7, 1):
@@ -355,9 +358,6 @@
     mine[1] = group
     for i, o in enumerate(ROW_PEERS):
         remote(mine.at[1], tot.at[i], 11, sts.at[1], row_at(*o)).start()
-    apart([(0, r, met(0, r, FAR[1])) for r in (3, 2)])
-    send_row(1, 3)
-    send_row(1, 2)
     apart([(1, p, met(1, p, range(NR // 2))) for p in (2, 6, 3, 4, 5)] + [(0, 0, HALF)])
     for p in (2, 6, 3, 4, 5):
         send_col(1, p)

time: 39 us -> 39.5 us (1.013)
  Pallas kernels: 37 us -> 37.5 us
    pallas_call x1, Pallas kernels: 37 us -> 37.5 us  [on_device(): pl.pallas_call(cg_kernel, out_shape=(out, out, out), in_specs=[hbm] * 5,...]
where the time goes in v8:
time: 39.5 us; the launch traced here: 39.4 us
  Pallas kernels  37.5 us (95%)
  between operations  1.3 us (3%)
  other arithmetic  0.61 us (2%)
    pallas_call x1, Pallas kernels, on_device(): pl.pallas_call(cg_kernel, out_shape=(out, out, out), in_specs=[hbm] * 5,...  37.5 us

profile of v8, /device:TPU:1, one launch (start us, length us, event | category | flops | bytes accessed | tf_op | source)
XLA Modules:
  0.0 39.4 jit_solution(13354877426921784652)
XLA Ops:
  1.3 0.0 copy-start
  1.3 37.5 %shard_map.76 = (f32[16,128]{1,0:T(8,128)S(1)}, f32[16,128]{1,0:T(8,128)S(1)}, f32[16,128]{1,0:T(8,128)S(1)}) custom-call(f32[8,128]{1,0:T(8,128)} %design_ref.1, f32[8]{0:T(128)} %scales_ref.1, s32[1,128]{1,0:T(1,128)} %bitcast.1, f32[1]{0:T(128)S(6)} %copy.8.noise_ref, f32[16,128]{1,0:T(8,128)} %targets_ref.1), custom_call_target="tpu_custom_call" | custom-call | tf_op jit(solution)/shard_map/pallas_call | solution.py:395
  38.8 0.0 copy-done
  38.8 0.6 %multiply_subtract_fusion = (f32[16,128]{1,0:T(8,128)}, f32[16,128]{1,0:T(8,128)}, f32[16,128]{1,0:T(8,128)}) fusion(f32[16,128]{1,0:T(8,128)S(1)} %get-tuple-element.7, f32[16,128]{1,0:T(8,128)S(1)} %get-tuple-element.6, f32[16,128]{1,0:T(8,128)S(1)} %get-tuple-element.8, f32[16,128]{1,0:T(8,128)S(1)} %copy-done), kind=kLoop, calls=%fused_computation | loop fusion | flops 10240 | bytes 57344 | tf_op jit(solution)/shard_map/sub | solution.py:414
Async XLA Ops:
  1.3 37.5 %copy-start = (f32[16,128]{1,0:T(8,128)S(1)}, f32[16,128]{1,0:T(8,128)}, u32[]{:S(2)}) copy-start(f32[16,128]{1,0:T(8,128)} %targets_ref.1) | copy-start | bytes 24580
